TPU v7x, 256 devices: a whole 4x4x8 slice. The times are simulated.
256 devices in a mesh: dp: 32 (over x, z), head: 8 (over y, core).
Axes of the slice: x: 4, y: 4, z: 8, core: 2. Of those that a mesh axis runs over, the one named last changes fastest.
Arguments:
- tokens: bfloat16 [16384, 4096], P('dp'), may hold values from -6 to 6
- q_weight: bfloat16 [4096, 8192], P('dp', 'head'), may hold values from -0.09375 to 0.09375
- kv_weight: bfloat16 [4096, 1024], P('dp', 'head'), may hold values from -0.09375 to 0.09375
- q_gain: float32 [128], replicated, may hold values from 0.1 to 1.9
- k_gain: float32 [128], replicated, may hold values from 0.1 to 1.9
- doc_lengths: int32 [32, 16], replicated, may hold values from 0 to 512, as said below
Outputs:
- attended: bfloat16 [16384, 8192], P('dp', 'head')
Inputs may be any that keep to these rules, and one draw needn't show every extreme that they name: `doc_lengths`: row r lists the lengths of the documents packed in order on index r of dp and sums to 512; some rank holds a single document of 512 tokens.
All inputs are finite; a program needn't handle non-finite values.
Results may differ from a plain program's by a relative error of at most 0.0068.
Values may be sent and summed in bfloat16 or wider, within the bound.
A program may use at most 64 MiB of HBM per device.

v0:
```python
import math

import jax
import jax.numpy as jnp
from jax import lax
from jax.sharding import PartitionSpec as P

KVH = 4
HD = 128


theta_base = 1000000.0
norm_eps = 1e-06


def doc_layout(lengths, count):
    doc_ends = jnp.cumsum(lengths)
    places = jnp.arange(count, dtype=jnp.int32)
    passed = (places[:, None] >= doc_ends[None, :]).astype(jnp.int32)
    doc_ids = jnp.sum(passed, axis=1)
    starts = jnp.sum(passed * lengths[None, :], axis=1)
    return (doc_ids, places - starts)


def norm_rope(raw, gain, positions):
    half_width = raw.shape[-1] // 2
    inv_rms = lax.rsqrt(jnp.mean(raw * raw, axis=-1, keepdims=True) + norm_eps)
    normed = raw * inv_rms * gain
    frequency = jnp.exp(
        jnp.arange(half_width, dtype=jnp.float32) * (-2.0 * math.log(theta_base) / raw.shape[-1])
    )
    angles = positions.astype(jnp.float32)[:, None] * frequency[None, :]
    cosine = jnp.cos(angles)[:, None, :]
    sine_table = jnp.sin(angles)[:, None, :]
    lower_half = normed[..., :half_width]
    second = normed[..., half_width:]
    return jnp.concatenate(
        [lower_half * cosine - second * sine_table, second * cosine + lower_half * sine_table],
        axis=-1,
    ).astype(jnp.bfloat16)


def shards(tokens, q_weight, kv_weight, q_gain, k_gain, doc_lengths):
    rows_here = tokens.shape[0]
    heads_here = q_weight.shape[1] // HD
    own_rank = lax.axis_index("dp")
    kv_all = lax.all_gather(kv_weight, "head", axis=1, tiled=True)
    kv_head = lax.axis_index("head") * KVH // lax.axis_size("head")
    key_cols = lax.dynamic_slice_in_dim(kv_all, kv_head * HD, HD, 1)
    value_cols = lax.dynamic_slice_in_dim(kv_all, (KVH + kv_head) * HD, HD, 1)
    pair_cols = jnp.concatenate([key_cols, value_cols], axis=1)

    def add_rows(shard_rows):
        return jnp.dot(tokens, shard_rows, preferred_element_type=jnp.float32)

    q_sum = add_rows(lax.all_gather(q_weight, "dp", axis=0, tiled=True))
    pair_sum = add_rows(lax.all_gather(pair_cols, "dp", axis=0, tiled=True))
    lengths = lax.dynamic_index_in_dim(doc_lengths, own_rank, 0, keepdims=False)
    doc_ids, positions = doc_layout(lengths, rows_here)
    places = jnp.arange(rows_here, dtype=jnp.int32)
    queries = norm_rope(q_sum.reshape(rows_here, heads_here, HD), q_gain, positions)
    key_rows = norm_rope(pair_sum[:, :HD].reshape(rows_here, 1, HD), k_gain, positions)[:, 0]
    values = pair_sum[:, HD:].astype(jnp.bfloat16)
    scores = jnp.einsum(
        "qhd,td->hqt", queries, key_rows, preferred_element_type=jnp.float32
    ) * HD ** (-0.5)
    allowed = (doc_ids[:, None] == doc_ids[None, :]) & (places[:, None] >= places[None, :])
    weights = jnp.where(allowed[None], jnp.exp(scores), 0.0)
    probs = (weights / jnp.sum(weights, axis=-1, keepdims=True)).astype(jnp.bfloat16)
    mixed_out = jnp.einsum("hqt,td->qhd", probs, values, preferred_element_type=jnp.float32)
    return mixed_out.astype(jnp.bfloat16).reshape(rows_here, heads_here * HD)


def solution(mesh):
    placed = (P("dp", None), P("dp", "head"), P("dp", "head"), P(), P(), P())
    return jax.shard_map(
        shards, mesh=mesh, in_specs=placed, out_specs=P("dp", "head"), check_vma=False
    )
```

profile of v0, /device:TPU:1, one launch (start us, length us, event | category | flops | bytes accessed | tf_op | source)
XLA Modules:
  0.0 222.3 jit_solution(3711025355796249315)
XLA Ops:
  6.5 0.0 all-gather.3.cloned.1.call-start
  6.5 14.7 %all_gather.9 = bf16[128,1024]{1,0:T(8,128)(2,1)S(1)} all-gather(bf16[128,128]{1,0:T(8,128)(2,1)} %param.8), channel_id=1, replica_groups=mesh['dp'=32,'head'=8] {'head'}, dimensions={1}, use_global_device_ids=true | all-gather | bytes 294912 | tf_op jit(solution)/shard_map/all_gather | solution.py:47
  21.3 0.6 pad_maximum_fusion
  21.9 0.0 all-gather.3.cloned.1.call-update
  22.0 0.0 all-gather.5.cloned.1.call-start
  22.0 0.7 all-gather.5.cloned.1.call-update
  22.7 0.9 dynamic-slice_reduce_fusion
  23.6 0.1 reduce.2
  23.8 0.1 convert_reduce_fusion
  23.9 0.9 fusion.8
  24.8 1.0 multiply_cosine_fusion
  25.8 0.0 copy-start.1
  25.8 70.1 %all-gather.3.cloned.1.call-done = bf16[4096,256]{1,0:T(8,128)(2,1)} async-done(((bf16[128,256]{1,0:T(8,128)(2,1)}), bf16[4096,256]{1,0:T(8,128)(2,1)}) %all-gather.3.cloned.1.call-update) | async-done | bytes 2097168 | tf_op jit(solution)/shard_map/all_gather | solution.py:57
  95.9 4.1 %convolution_bitcast_fusion = f32[512,256]{0,1:T(8,128)S(1)} fusion(bf16[4096,256]{1,0:T(8,128)(2,1)} %all-gather.3.cloned.1.call-done, bf16[512,4096]{1,0:T(8,128)(2,1)} %param.6), kind=kOutput, calls=%fused_computation.10 | convolution fusion | flops 1073741824 | bytes 6815744 | tf_op jit(solution)/shard_map/dot_general | solution.py:54
  100.1 0.0 copy-done.1
  100.1 0.1 multiply_bitcast_fusion
  100.2 0.6 fusion.22
  100.7 96.7 %all-gather.5.cloned.1.call-done = bf16[4096,1024]{1,0:T(8,128)(2,1)} async-done(((bf16[128,1024]{1,0:T(8,128)(2,1)}), bf16[4096,1024]{1,0:T(8,128)(2,1)}) %all-gather.5.cloned.1.call-update) | async-done | bytes 8388624 | tf_op jit(solution)/shard_map/all_gather | solution.py:56
  197.4 8.1 %fusion.26 = f32[512,1024]{1,0:T(8,128)S(1)} fusion(bf16[512,4096]{1,0:T(8,128)(2,1)} %param.6, bf16[4096,1024]{1,0:T(8,128)(2,1)} %all-gather.5.cloned.1.call-done), kind=kOutput, calls=%fused_computation.53 | convolution fusion | flops 4294967296 | bytes 14680064 | tf_op jit(solution)/shard_map/dot_general | solution.py:54
  205.6 0.5 copy.39
  206.1 0.6 multiply_reduce_fusion
  206.7 0.1 copy.30
  206.8 1.4 fusion.2
  208.2 0.0 copy-start
  208.2 0.8 subtract_convert_fusion
  209.0 0.2 copy-done
  209.1 2.6 %fusion = (f32[8,512]{1,0:T(8,128)S(1)}, f32[512,512,8]{1,0,2:T(8,128)S(1)}) fusion(pred[512,512]{0,1:T(8,128)(4,1)S(1)} %copy-done, bf16[512,8,64]{2,0,1:T(8,128)(2,1)S(1)} %get-tuple-element.8, bf16[512,8,64]{2,0,1:T(8,128)(2,1)S(1)} %get-tuple-element.7, bf16[512,64]{0,1:T(8,128)(2,1)S(1)} %get-tuple-element.10, bf16[512,64]{0,1:T(8,128)(2,1)S(1)} %get-tuple-element.9), kind=kOutput, calls=%fused_computation.2 | convolution fusion | flops 545517568 | bytes 9846784 | tf_op jit(solution)/shard_map/qhd,td->hqt/dot_general | solution.py:64
  211.7 2.4 %fusion.3 = bf16[128,8,512]{2,0,1:T(8,128)(2,1)S(1)} fusion(f32[512,512,8]{1,0,2:T(8,128)S(1)} %get-tuple-element.18, f32[8,512]{1,0:T(8,128)S(1)} %get-tuple-element.17, pred[512,512]{0,1:T(8,128)(4,1)S(1)} %copy-done, f32[512,256]{0,1:T(8,128)S(1)} %convolution_bitcast_fusion), kind=kOutput, calls=%fused_computation.9 | convolution fusion | flops 545783808 | bytes 9846784 | tf_op jit(solution)/shard_map/hqt,td->qhd/dot_general | solution.py:70
  214.1 1.3 copy.34
  (7 shorter events, 0.1 us)
Async XLA Ops:
  6.5 89.3 %all-gather.3.cloned.1.call-start = ((), (), s32[]{:S(2)}) async-start(), calls=%async_computation | async-start | bytes 2162688 | tf_op jit(solution)/shard_map/all_gather | solution.py:57
  22.0 175.5 %all-gather.5.cloned.1.call-start = ((), (), s32[]{:S(2)}) async-start(), calls=%async_computation.1 | async-start | bytes 8650752 | tf_op jit(solution)/shard_map/all_gather | solution.py:56
  25.8 74.3 %copy-start.1 = (f32[128]{0:T(128)S(1)}, f32[128]{0:T(128)}, u32[]{:S(2)}) copy-start(f32[128]{0:T(128)} %param.10) | copy-start | bytes 1540
  208.2 1.0 copy-start
Sparse Core Ops, SparseCore 0:
  22.1 73.7 all-gather.2
  98.5 98.9 all-gather.4
where the time goes:
time: 222 us
  waiting for transfers between devices  168 us (76%)
  matrix products  17.3 us (8%)
  blocking collectives  14.7 us (7%)
  between operations  13.5 us (6%)
  other arithmetic  6.22 us (3%)
  local copies, waits for them, and re-layouts  2.96 us (1%)
    all_gather x1, waiting for transfers between devices, shards(): q_sum = add_rows(lax.all_gather(q_weight, 'dp', axis=0, tiled=True))  96.7 us
    all_gather x1, waiting for transfers between devices, shards(): pair_sum = add_rows(lax.all_gather(pair_cols, 'dp', axis=0, tiled=True))  70.1 us
    all_gather x1, blocking collectives, shards(): kv_all = lax.all_gather(kv_weight, 'head', axis=1, tiled=True)  14.7 us
    dot_general x2, matrix products, add_rows(): return jnp.dot(tokens, shard_rows, preferred_element_type=jnp.float32)  12.3 us
  transfers between devices with their start and end apart: 2, of which 2 were waited for; matrix products, arithmetic and copies ran while one was open for 4% of the time, Pallas kernels for 0%

commit v1 on v0

v1 whole, which is shorter than its diff:
```python
import functools
import math

import jax
import jax.numpy as jnp
import numpy as np
from jax import lax
from jax.experimental import pallas as pl
from jax.experimental.pallas import tpu as pltpu
from jax.sharding import PartitionSpec as P

HD = 128
ROWS = 512
FEAT = 4096
THETA = 1000000.0
EPS = 1e-06
MESH = pl.DeviceIdType.MESH
F32 = jnp.float32
BF16 = jnp.bfloat16
N_SEND = 224
GROUPS = (0, 1, 2)
OWN, NEAR, PAIR, FAR = 0, 1, 2, 3


def kernel(tok, w, kvw, qg, kg, freq, dl, out,
           tokb, wbuf, kvbuf, acc, kvacc, kvst, kvin, cosb, sinb, bias, ost,
           send, rw, rt, rs, rkv, rout, loc):
    dp = lax.axis_index("dp")
    hd = lax.axis_index("head")
    x, z = dp // 8, dp % 8
    y, c = hd // 2, hd % 2
    side = x // 2
    xn, xp = x + 1 - 2 * (x % 2), 3 - x
    worker = c == side
    is_v = y // 2
    kv_to = 2 * (y % 2) + side

    def dev(xx, zz, yy, cc):
        return (xx * 8 + zz, yy * 2 + cc)

    near = dev(xn, z, y, c)
    pair = dev(xp, z, y, c)
    up, down = dev(x, (z + 1) % 8, y, c), dev(x, (z + 7) % 8, y, c)
    yup, ydown = dev(x, z, (y + 1) % 4, c), dev(x, z, (y + 3) % 4, c)
    sib = dev(x, z, y, 1 - c)

    barrier = pltpu.get_barrier_semaphore()
    for peer in (near, pair, up, down, yup, ydown, sib):
        pl.semaphore_signal(barrier, inc=1, device_id=peer, device_id_type=MESH)
    src_side = y % 2
    src_x = jnp.where(side == src_side, x, xp)
    kv_self = worker & (kv_to == y)
    for v in (0, 1):
        src_y = 2 * v + y // 2
        @pl.when(jnp.logical_not(kv_self & (is_v == v)))
        def _():
            pl.semaphore_signal(
                barrier, inc=1, device_id=dev(src_x, z, src_y, src_side), device_id_type=MESH)
    extra = jnp.where(worker, jnp.where(kv_to == y, 3, 4), 0)
    pl.semaphore_wait(barrier, 7 + extra)

    used = [0]
    pending = {"all": [], "worker": [], "helper": [], "beyond": []}

    def push(src, dst, rsem, to, who="all"):
        n = used[0]
        used[0] += 1
        pending[who].append((n, dst))
        pltpu.make_async_remote_copy(
            src_ref=src(), dst_ref=dst(), send_sem=send.at[n], recv_sem=rsem,
            device_id=to, device_id_type=MESH).start()

    def drain(who):
        for n, dst in pending[who]:
            arrive(dst(), send.at[n])

    def arrive(dst, rsem):
        pltpu.make_async_copy(dst, dst, rsem).wait()

    def slot(g, q, xi):
        at, lo, n = (q, 0, 128) if q < 7 else (7, 64 * (q - 7), 64)
        buf = kvbuf if g == 0 else wbuf.at[g - 1]
        return buf.at[at, pl.ds(xi * 128 + lo, n), :]

    def half(g, q, xi, h):
        buf = kvbuf if g == 0 else wbuf.at[g - 1]
        return buf.at[q, pl.ds(xi * 128 + 64 * h, 64), :]

    def source(g, of_side):
        if g == 0:
            return kvw
        return w.at[:, pl.ds(pl.multiple_of(of_side * 512 + (g - 1) * 256, 256), 256)]

    def guarded(g, fn):
        if g == 0:
            pl.when(worker)(fn)
        else:
            fn()

    def who(g):
        return "worker" if g == 0 else "all"

    def wait_w(g, q, xi):
        arrive(slot(g, q, xi), rw.at[g, q, xi])

    def ring_first(g, xi, src):
        push(src, lambda: slot(g, 1, xi), rw.at[g, 1, xi], up, who(g))
        push(src, lambda: slot(g, 2, xi), rw.at[g, 2, xi], down, who(g))

    def cross(g, q):
        push(lambda: slot(g, q, PAIR), lambda: slot(g, q, FAR), rw.at[g, q, FAR], near, who(g))

    def start_pair(g):
        if g == 0:
            @pl.when(jnp.logical_not(worker))
            def _():
                push(lambda: kvw, lambda: slot(0, 0, PAIR), rw.at[0, 0, PAIR], pair, "helper")
        else:
            push(lambda: source(g, 1 - side), lambda: slot(g, 0, PAIR), rw.at[g, 0, PAIR], pair)

    def start_near(g):
        guarded(g, lambda: push(lambda: source(g, side), lambda: slot(g, 0, NEAR), rw.at[g, 0, NEAR], near, who(g)))

    def start_own(g):
        guarded(g, lambda: ring_first(g, OWN, lambda: source(g, side)))

    def begin_near(g):
        def go():
            wait_w(g, 0, NEAR)
            ring_first(g, NEAR, lambda: slot(g, 0, NEAR))
        guarded(g, go)

    def begin_pair(g):
        def go():
            wait_w(g, 0, PAIR)
            ring_first(g, PAIR, lambda: slot(g, 0, PAIR))
            cross(g, 0)
        guarded(g, go)

    def ring(g, k, items=(PAIR, OWN, NEAR)):
        def go():
            for xi in items:
                for d in (0, 1):
                    q = 2 * k - 1 + d
                    wait_w(g, q, xi)
                    to = (up, down)[d]
                    if k < 3:
                        push(lambda: slot(g, q, xi), lambda q=q, xi=xi: slot(g, q + 2, xi), rw.at[g, q + 2, xi], to, who(g))
                    elif k == 3:
                        push(lambda: half(g, q, xi, d), lambda d=d, xi=xi: slot(g, 7 + d, xi), rw.at[g, 7 + d, xi], to, who(g))
                    if xi == PAIR:
                        cross(g, q)
        guarded(g, go)

    def far(g, qs):
        def go():
            for q in qs:
                wait_w(g, q, FAR)
        guarded(g, go)

    def cols(head_of):
        return pl.ds(pl.multiple_of(head_of * 512, 512), 512)

    def piece(j, head_of):
        return tokb.at[1, pl.ds(128 * j, 128), cols(head_of)]

    y_of = ((y) % 4, (y + 3) % 4, (y + 1) % 4, (y + 2) % 4)

    def tok_mine(j):
        ref = lambda: piece(j, hd)
        arrive(ref(), rt.at[0, j])
        push(ref, ref, rt.at[1, j], yup)
        push(ref, ref, rt.at[2, j], ydown)
        push(ref, ref, rs.at[0, j], sib)

    def tok_side(src, j):
        ref = lambda: piece(j, y_of[src] * 2 + c)
        arrive(ref(), rt.at[src, j])
        if src == 1 and j < 2:
            push(ref, ref, rt.at[3, j], yup)
        if src == 2 and j >= 2:
            push(ref, ref, rt.at[3, j], ydown)
        push(ref, ref, rs.at[src, j], sib)

    def tok_sib():
        for src in range(4):
            for j in range(4):
                arrive(piece(j, y_of[src] * 2 + 1 - c), rs.at[src, j])

    start_pair(0)
    start_pair(1)
    start_near(0)
    start_own(0)
    start_near(1)
    start_own(1)
    for j in (0, 1):
        push(lambda: tok.at[pl.ds(128 * j, 128), cols(hd)], lambda j=j: piece(j, hd), rt.at[0, j], pair)
    start_pair(2)
    for j in (2, 3):
        push(lambda: tok.at[pl.ds(128 * j, 128), cols(hd)], lambda j=j: piece(j, hd), rt.at[0, j], pair)
    start_near(2)

    load_tok = pltpu.make_async_copy(tok, tokb.at[0], loc.at[0])
    load_tok.start()
    load_w = []
    for g in (1, 2):
        load_w.append(pltpu.make_async_copy(source(g, side), slot(g, 0, OWN), loc.at[g]))
        load_w[-1].start()
    load_kv = pltpu.make_async_copy(kvw, slot(0, 0, OWN), loc.at[3])
    load_kv.start()

    def tables(t):
        rank = dp if t == 0 else xp * 8 + z
        row = lax.broadcasted_iota(jnp.int32, (ROWS, HD), 0)
        lane = lax.broadcasted_iota(jnp.int32, (ROWS, HD), 1)
        start = jnp.zeros((ROWS, HD), jnp.int32)
        end = 0
        for d in range(16):
            n = dl[rank, d]
            end = end + n
            start = start + jnp.where(row >= end, n, 0)
        angle = (row - start).astype(F32) * freq[...]
        cosb[t] = jnp.cos(angle)
        s = jnp.sin(angle)
        sinb[t] = jnp.where(lane < 64, -s, s)
        for j in range(4):
            col = lane + 128 * j
            bias[t, :, 128 * j:128 * j + 128] = jnp.where(
                (col >= start) & (col <= row), 0.0, -1e30)

    def norm_rope(u, gain, t):
        ms = jnp.mean(u * u, axis=-1, keepdims=True)
        n = u * lax.rsqrt(ms + EPS) * gain
        return (n * cosb[t] + pltpu.roll(n, 64, 1) * sinb[t]).astype(BF16)

    def lhs(t, p):
        k = (p + 1) // 2
        zz = (z + 8 + k - 2 * k * (p % 2)) % 8
        parts = []
        for xx in (x, xn, xp, 3 - xn):
            f = pl.multiple_of((xx * 8 + zz) * 128, 128)
            parts.append(tokb[t, :, pl.ds(f, 128)])
        return jnp.concatenate(parts, axis=1)

    def dots(t, ps, gs=(1, 2)):
        def body(p, _):
            a = lhs(t, p)
            for g in gs:
                acc[t, g - 1] += jnp.dot(a, wbuf[g - 1, p], preferred_element_type=F32)
            return 0
        lax.fori_loop(ps[0], ps[1], body, 0)

    def kv_product(t):
        @pl.when(worker)
        def _():
            kvacc[...] = jnp.zeros_like(kvacc)

            def body(p, _):
                kvacc[...] += jnp.dot(lhs(t, p), kvbuf[p], preferred_element_type=F32)
                return 0
            lax.fori_loop(0, 8, body, 0)

            @pl.when(is_v == 0)
            def _():
                kvst[t] = norm_rope(kvacc[...], kg[...], t)

            @pl.when(is_v == 1)
            def _():
                kvst[t] = kvacc[...].astype(BF16)

    def kv_send(t):
        @pl.when(worker)
        def _():
            for xx, tt in ((x, t), (xp, 1 - t)):
                def send_to(core, kind):
                    push(lambda: kvst.at[t], lambda tt=tt: kvin.at[is_v, tt],
                         rkv.at[is_v, tt], dev(xx, z, kv_to, core), kind)
                send_to(1 - c, "worker")
                if tt != t:
                    send_to(c, "worker")
                    continue
                pl.when(kv_to != y)(lambda: send_to(c, "beyond"))

                @pl.when(kv_to == y)
                def _():
                    pltpu.make_async_copy(kvst.at[t], kvin.at[is_v, t], rkv.at[is_v, t]).start()

    scale = HD ** -0.5 * math.log2(math.e)

    def attend(t, g, hh):
        q = norm_rope(acc[t, g - 1, :, 128 * hh:128 * hh + 128], qg[...], t)
        for i in (0, 1):
            m = 256 * (i + 1)
            s = lax.dot_general(q[256 * i:m], kvin[0, t, :m], (((1,), (1,)), ((), ())),
                                preferred_element_type=F32)
            e = jnp.exp2(s * scale + bias[t, 256 * i:m, :m])
            probs = (e * (1.0 / jnp.sum(e, axis=-1, keepdims=True))).astype(BF16)
            o = jnp.dot(probs, kvin[1, t, :m], preferred_element_type=F32)
            ost[t, 256 * i:m, (g - 1) * 256 + 128 * hh:(g - 1) * 256 + 128 * hh + 128] = o.astype(BF16)

    def emit(t, g):
        here = ost.at[t, :, pl.ds(256 * (g - 1), 256)]
        there = out.at[:, pl.ds(pl.multiple_of(side * 512 + 256 * (g - 1), 256), 256)]
        if t == 1:
            push(lambda: here, lambda: there, rout.at[g - 1], pair)
        else:
            pltpu.make_async_copy(here, there, loc.at[3 + g]).start()

    acc[...] = jnp.zeros_like(acc)
    begin_near(0)
    begin_pair(0)
    begin_near(1)
    begin_pair(1)
    tables(0)
    ring(0, 1)
    start_own(2)
    tok_mine(0)
    ring(0, 2)
    begin_near(2)
    tok_mine(1)
    tables(1)
    ring(0, 3)
    begin_pair(2)
    tok_mine(2)
    ring(1, 1)
    ring(0, 4)
    tok_mine(3)
    for j in (0, 1):
        tok_side(1, j)
        tok_side(2, j)
    load_tok.wait()
    load_kv.wait()
    for cp in load_w:
        cp.wait()
    far(0, range(9))
    kv_product(0)
    kv_send(0)
    ring(2, 1)
    for j in (2, 3):
        tok_side(1, j)
        tok_side(2, j)
    far(1, (0,))
    far(2, (0,))
    dots(0, (0, 1))
    ring(1, 2)
    for j in range(4):
        tok_side(3, j)
    far(1, (1, 2))
    far(2, (1, 2))
    dots(0, (1, 3))
    ring(2, 2)
    tok_sib()
    kv_product(1)
    kv_send(1)
    far(1, (3, 4))
    far(2, (3, 4))
    dots(0, (3, 5))
    dots(1, (0, 5))
    ring(1, 3)
    ring(2, 3)
    ring(1, 4, (PAIR,))
    ring(2, 4, (PAIR,))
    far(1, (5, 6))
    far(2, (5, 6))
    dots(0, (5, 7))
    dots(1, (5, 7))
    ring(1, 4, (OWN, NEAR))
    far(1, (7, 8))
    dots(1, (7, 8), (1,))
    dots(0, (7, 8), (1,))
    for v in (0, 1):
        for t in (1, 0):
            arrive(kvin.at[v, t], rkv.at[v, t])
    for hh in (0, 1):
        attend(1, 1, hh)
    for hh in (0, 1):
        attend(0, 1, hh)
    emit(1, 1)
    emit(0, 1)
    ring(2, 4, (OWN, NEAR))
    far(2, (7, 8))
    dots(1, (7, 8), (2,))
    for hh in (0, 1):
        attend(1, 2, hh)
    dots(0, (7, 8), (2,))
    emit(1, 2)
    for hh in (0, 1):
        attend(0, 2, hh)
    emit(0, 2)

    drain("all")
    pl.when(worker)(lambda: drain("worker"))
    pl.when(worker & (kv_to != y))(lambda: drain("beyond"))
    pl.when(jnp.logical_not(worker))(lambda: drain("helper"))
    for g in (1, 2):
        here = ost.at[0, :, pl.ds(256 * (g - 1), 256)]
        there = out.at[:, pl.ds(pl.multiple_of(side * 512 + 256 * (g - 1), 256), 256)]
        pltpu.make_async_copy(here, there, loc.at[3 + g]).wait()
        other = out.at[:, pl.ds(pl.multiple_of((1 - side) * 512 + 256 * (g - 1), 256), 256)]
        arrive(other, rout.at[g - 1])
    assert used[0] <= N_SEND, used[0]


def shards(tokens, q_weight, kv_weight, q_gain, k_gain, doc_lengths):
    half = np.exp(np.arange(64) * (-2.0 * math.log(THETA) / HD)).astype(np.float32)
    freq = jnp.asarray(np.concatenate([half, half])[None, :])
    vm = pl.BlockSpec(memory_space=pltpu.VMEM)
    any_ = pl.BlockSpec(memory_space=pl.ANY)
    dma = pltpu.SemaphoreType.DMA
    return pl.pallas_call(
        kernel,
        out_shape=jax.ShapeDtypeStruct((ROWS, 1024), BF16),
        in_specs=[any_, any_, any_, vm, vm, vm, pl.BlockSpec(memory_space=pltpu.SMEM)],
        out_specs=any_,
        scratch_shapes=[
            pltpu.VMEM((2, ROWS, FEAT), BF16),
            pltpu.VMEM((2, 8, 512, 256), BF16),
            pltpu.VMEM((8, 512, 128), BF16),
            pltpu.VMEM((2, 2, ROWS, 256), F32),
            pltpu.VMEM((ROWS, 128), F32),
            pltpu.VMEM((2, ROWS, 128), BF16),
            pltpu.VMEM((2, 2, ROWS, 128), BF16),
            pltpu.VMEM((2, ROWS, HD), F32),
            pltpu.VMEM((2, ROWS, HD), F32),
            pltpu.VMEM((2, ROWS, ROWS), F32),
            pltpu.VMEM((2, ROWS, 512), BF16),
            dma((N_SEND,)),
            dma((3, 9, 4)),
            dma((4, 4)),
            dma((4, 4)),
            dma((2, 2)),
            dma((2,)),
            dma((6,)),
        ],
        compiler_params=pltpu.CompilerParams(
            collective_id=0, has_side_effects=True, vmem_limit_bytes=60 * 2**20),
        cost_estimate=pl.CostEstimate(
            flops=6_000_000_000, bytes_accessed=12 * 2**20, transcendentals=2**21),
    )(tokens, q_weight, kv_weight, q_gain[None, :], k_gain[None, :], freq, doc_lengths)


def solution(mesh):
    placed = (P("dp", None), P("dp", "head"), P("dp", "head"), P(), P(), P())
    return jax.shard_map(
        shards, mesh=mesh, in_specs=placed, out_specs=P("dp", "head"), check_vma=False
    )
```

time: 222 us -> 80 us (0.36)
  the two profiles are of different devices: /device:TPU:1 before, /device:TPU:2 now
where the time goes in v1:
time: 80 us; the launch traced here: 79.8 us
  Pallas kernels  76.1 us (95%)
  local copies, waits for them, and re-layouts  3.64 us (5%)
    pallas_call x1, Pallas kernels, shards(): pl.pallas_call(kernel, out_shape=jax.ShapeDtypeStruct((ROWS, 1024), BF16)...  76.1 us
    unnamed x2, local copies, waits for them, and re-layouts  3.64 us

profile of v1, /device:TPU:2, one launch (start us, length us, event | category | flops | bytes accessed | tf_op | source)
XLA Modules:
  0.0 79.8 jit_solution(1848251407042137815)
XLA Ops:
  0.0 1.4 %copy.8.dl = s32[32,16]{1,0:T(8,128)} copy(s32[32,16]{0,1:T(8,128)} %param.12) | data formatting | bytes 4096 | tf_op args[5]
  1.4 76.1 %shard_map.73 = bf16[512,1024]{1,0:T(8,128)(2,1)} custom-call(bf16[512,4096]{1,0:T(8,128)(2,1)} %tok.1, bf16[128,1024]{1,0:T(8,128)(2,1)} %w.1, bf16[128,128]{1,0:T(8,128)(2,1)} %kvw.1, f32[1,128]{1,0:T(1,128)} %bitcast.2, f32[1,128]{1,0:T(1,128)} %bitcast.3, f32[1,128]{1,0:T(1,128)} %constant.2.clone.freq, s32[32,16]{1,0:T(8,128)} %copy.8.dl), custom_call_target="tpu_custom_call" | custom-call | flops 6000000000 | bytes 12582912 | tf_op jit(solution)/shard_map/pallas_call | solution.py:410
  77.5 2.3 %copy.10 = bf16[512,1024]{1,0:T(8,128)(2,1)} copy(bf16[512,1024]{1,0:T(8,128)(2,1)} %shard_map.73) | data formatting | bytes 2097152

commit v2 on v0

v2 whole, which is shorter than its diff:
```python
import functools
import math

import jax
import jax.numpy as jnp
import numpy as np
from jax import lax
from jax.experimental import pallas as pl
from jax.experimental.pallas import tpu as pltpu
from jax.sharding import PartitionSpec as P

HD = 128
ROWS = 512
FEAT = 4096
THETA = 1000000.0
EPS = 1e-06
MESH = pl.DeviceIdType.MESH
F32 = jnp.float32
BF16 = jnp.bfloat16
S_KV, S_HELP, S_TOK, S_KEYS, S_BEYOND, S_OUT, S_SHARE = 0, 3, 4, 5, 6, 7, 8
GROUPS = (0, 1, 2)
OWN, NEAR, PAIR, FAR = 0, 1, 2, 3


PIECE = 64
RELAYED = 2

ORDER = (
    ("pair",0), ("pair",1), ("tokp",0), ("tokp",1), ("pair",2), ("tokp",2), ("tokp",3), ("tokp",4),
    ("tokp",5), ("tokp",6), ("tokp",7), ("tokp2",4), ("tokp2",5), ("tokp2",6), ("tokp2",7), ("near",0),
    ("near",1), ("near",2), ("src",0,0), ("tables",0), ("src",1,0), ("src",2,0), ("tables",1), ("w",0,0,2),
    ("src",0,2), ("w",0,0,1), ("src",0,1), ("w",0,1,0), ("w",0,2,0), ("w",1,0,2), ("src",1,2), ("w",1,0,1),
    ("w",1,1,0), ("w",1,2,0), ("t",0,0), ("w",2,0,1), ("w",2,1,0), ("w",2,2,0), ("w",0,0,3), ("w",0,1,2),
    ("w",0,2,2), ("w",0,1,1), ("w",0,2,1), ("w",0,3,0), ("w",0,4,0), ("t",0,1), ("sib",0,0), ("w",1,0,3),
    ("w",1,1,2), ("w",1,2,2), ("s",0,0), ("w",2,0,2), ("w",0,1,3), ("w",0,2,3), ("t",1,0), ("t",2,0),
    ("w",1,3,0), ("w",1,4,0), ("t",0,2), ("t",1,1), ("sib",1,0), ("t",2,1), ("sib",2,0), ("w",2,3,0),
    ("w",2,4,0), ("t",0,3), ("sib",0,1), ("w",0,3,2), ("w",0,4,2), ("w",0,3,1), ("w",0,4,1), ("w",1,1,3),
    ("w",0,5,0), ("w",0,6,0), ("s",1,0), ("s",2,0), ("t",0,4), ("s",0,1), ("t",3,0), ("w",1,2,3),
    ("src",1,1), ("w",1,3,2), ("w",1,4,2), ("t",2,2), ("t",0,5), ("sib",0,2), ("t",1,2), ("w",2,0,3),
    ("w",1,5,0), ("w",1,6,0), ("t",2,3), ("sib",2,1), ("w",0,3,3), ("w",0,4,3), ("dots",0,(0,1,2,3,4),0),
    ("s",0,2), ("t",0,6), ("t",3,1), ("sib",3,0), ("w",2,5,0), ("w",2,6,0), ("s",2,1), ("t",2,4),
    ("w",0,5,2), ("w",0,6,2), ("t",0,7), ("sib",0,3), ("w",0,5,1), ("w",0,6,1), ("w",0,7,0), ("w",0,8,0),
    ("w",1,3,3), ("t",1,3), ("sib",1,1), ("s",3,0), ("t",3,2), ("src",2,2), ("s",0,3), ("t",3,4),
    ("w",1,1,1), ("w",1,2,1), ("dots",0,(0,1,2),1), ("w",1,4,3), ("s",1,1), ("t",1,4), ("t",2,5),
    ("sib",2,2), ("w",0,5,3), ("w",0,6,3), ("dots",0,(5,6),0), ("t",3,5), ("sib",3,2), ("w",1,5,2),
    ("w",1,6,2), ("t",1,5), ("sib",1,2), ("s",2,2), ("t",3,3), ("sib",3,1), ("w",1,7,0), ("w",1,8,0),
    ("t",3,6), ("w",2,7,0), ("w",2,8,0), ("src",2,1), ("s",3,2), ("w",0,7,2), ("w",0,8,2), ("t",1,6),
    ("w",0,7,1), ("w",0,8,1), ("s",1,2), ("t",2,6), ("s",3,1), ("t",3,7), ("sib",3,3), ("t",1,7),
    ("sib",1,3), ("w",2,1,2), ("w",2,2,2), ("t",2,7), ("sib",2,3), ("w",1,5,3), ("s",3,3), ("s",1,3),
    ("w",1,3,1), ("w",1,4,1), ("dots",0,(3,4),1), ("s",2,3), ("dots",1,(0,1,2,3,4,5,6),0), ("w",1,6,3),
    ("w",1,7,2), ("w",1,8,2), ("w",0,7,3), ("w",0,8,3), ("dots",1,(7,),0), ("kv",1), ("w",2,1,1),
    ("w",2,2,1), ("w",2,1,3), ("dots",0,(7,),0), ("kv",0), ("dots",1,(0,1,2,3,4),1), ("w",2,3,2),
    ("w",2,4,2), ("w",2,2,3), ("dots",0,(0,1,2),2), ("w",1,7,3), ("w",1,5,1), ("w",1,6,1),
    ("dots",1,(5,6),1), ("dots",0,(5,6),1), ("w",1,8,3), ("w",2,3,1), ("w",2,4,1), ("w",2,5,2), ("w",2,3,3),
    ("w",2,6,2), ("w",1,7,1), ("w",1,8,1), ("dots",1,(7,),1), ("dots",0,(7,),1), ("kvin",1), ("att",1,1,0),
    ("w",2,4,3), ("att",1,1,1), ("w",2,5,1), ("w",2,6,1), ("dots",1,(0,1,2,3,4),2), ("kvin",0), ("w",2,7,2),
    ("w",2,8,2), ("dots",0,(3,4),2), ("w",2,5,3), ("att",0,1,0), ("att",0,1,1), ("w",2,6,3),
    ("dots",1,(5,6),2), ("w",2,7,1), ("w",2,8,1), ("dots",0,(5,6),2), ("w",2,7,3), ("w",2,8,3),
    ("dots",1,(7,),2), ("att",1,2,0), ("att",1,2,1), ("dots",0,(7,),2), ("att",0,2,0), ("att",0,2,1),
)


def kernel(tok, w, kvw, qg_in, kg_in, freq_in, dl_in, out,
           tokb, wbuf, kvbuf, stage, acc, kvacc, kvst, kvin, cosb, sinb, bias, ost, qg, kg, freq, dl,
           send, rw, rt, rs, rkv, rout, loc):
    dp = lax.axis_index("dp")
    hd = lax.axis_index("head")
    x, z = dp // 8, dp % 8
    y, c = hd // 2, hd % 2
    side = x // 2
    xn, xp = x + 1 - 2 * (x % 2), 3 - x
    worker = c == side
    is_v = y // 2
    kv_to = 2 * (y % 2) + side

    def dev(xx, zz, yy, cc):
        return (xx * 8 + zz, yy * 2 + cc)

    near = dev(xn, z, y, c)
    pair = dev(xp, z, y, c)
    up, down = dev(x, (z + 1) % 8, y, c), dev(x, (z + 7) % 8, y, c)
    yup, ydown = dev(x, z, (y + 1) % 4, c), dev(x, z, (y + 3) % 4, c)
    sib = dev(x, z, y, 1 - c)

    small = [pltpu.make_async_copy(a, b, loc.at[4 + n])
             for n, (a, b) in enumerate(((qg_in, qg), (kg_in, kg), (freq_in, freq), (dl_in, dl)))]

    def columns(of_side, g):
        return w.at[:, pl.ds(pl.multiple_of(of_side * 512 + (g - 1) * 256, 256), 256)]

    load_kv = pltpu.make_async_copy(kvw, kvbuf.at[0], loc.at[1])
    load_kv.start()
    for g in (1, 2):
        pltpu.make_async_copy(columns(side, g), wbuf.at[g - 1, 0], loc.at[2]).start()
        pltpu.make_async_copy(columns(1 - side, g), stage.at[g - 1], loc.at[2]).start()
    load_tok = pltpu.make_async_copy(tok, tokb.at[0], loc.at[0])
    load_tok.start()
    for copy in small:
        copy.start()

    barrier = pltpu.get_barrier_semaphore()
    for peer in (near, pair, up, down, yup, ydown, sib):
        pl.semaphore_signal(barrier, inc=1, device_id=peer, device_id_type=MESH)
    src_side = y % 2
    src_x = jnp.where(side == src_side, x, xp)
    kv_self = worker & (kv_to == y)
    for v in (0, 1):
        src_y = 2 * v + y // 2
        @pl.when((c == src_side) & jnp.logical_not(kv_self & (is_v == v)))
        def _():
            pl.semaphore_signal(
                barrier, inc=1, device_id=dev(src_x, z, src_y, src_side), device_id_type=MESH)
    extra = jnp.where(worker, jnp.where(kv_to == y, 1, 2), 0)
    pl.semaphore_wait(barrier, 7 + extra)

    def push(src, dst, rsem, to, sid):
        pltpu.make_async_remote_copy(
            src_ref=src, dst_ref=dst, send_sem=send.at[sid], recv_sem=rsem,
            device_id=to, device_id_type=MESH).start()

    def arrive(dst, sem):
        pltpu.make_async_copy(dst, dst, sem).wait()

    def group(g):
        return kvbuf if g == 0 else wbuf.at[g - 1]

    def slot(g, q, xi):
        if q < 7:
            return group(g).at[4 * q + xi]
        return group(g).at[28 + xi, pl.ds(64 * (q - 7), 64), :]

    def half(g, q, xi, h):
        return group(g).at[4 * q + xi, pl.ds(64 * h, 64), :]

    def place(g, q, xi):
        if xi == FAR:
            n, blocks = ((23, 3),) * 3 + ((24, 2),) * 2 + ((25, 2),) * 2 + ((26, 1),) * 2, None
            n, blocks = n[q]
            copies = 2 if blocks == 1 else blocks
        elif xi != PAIR and q >= 7:
            n, blocks, copies = 22, 2, 4
        else:
            n, blocks, copies = (q - 1, q + 6, q + 13)[xi], 1, 1
        return rw.at[g, n], n, blocks, copies

    def rsem_of(g, q, xi):
        return place(g, q, xi)[0]

    def guarded(g, fn):
        if g == 0:
            pl.when(worker)(fn)
        else:
            fn()

    arrivals = {}

    def counted(key, copies):
        arrivals[key] = arrivals.get(key, 0) + 1
        return arrivals[key] == copies

    def wait_w(g, q, xi):
        sem, n, blocks, copies = place(g, q, xi)
        if copies == 1:
            arrive(slot(g, q, xi), sem)
        elif counted((g, n), copies):
            arrive(group(g).at[pl.ds(0, blocks)], sem)

    def ring_start(g, xi):
        def go():
            for d, to in ((1, up), (2, down)):
                push(slot(g, 0, xi), slot(g, d, xi), rsem_of(g, d, xi), to, g)
        guarded(g, go)

    def cross(g, q):
        push(slot(g, q, PAIR), slot(g, q, FAR), rsem_of(g, q, FAR), near, g)

    def start_pair(g):
        if g == 0:
            @pl.when(jnp.logical_not(worker))
            def _():
                push(slot(0, 0, OWN), slot(0, 0, PAIR), rsem_of(0, 0, PAIR), pair, S_HELP)
        else:
            push(stage.at[g - 1], slot(g, 0, PAIR), rsem_of(g, 0, PAIR), pair, g)

    def start_near(g):
        def go():
            push(slot(g, 0, OWN), slot(g, 0, NEAR), rsem_of(g, 0, NEAR), near, g)
        guarded(g, go)

    def cols(head_of):
        return pl.ds(pl.multiple_of(head_of * 512, 512), 512)

    def piece(j, head_of):
        return tokb.at[1, pl.ds(PIECE * j, PIECE), cols(head_of)]

    y_of = (y, (y + 3) % 4, (y + 1) % 4, (y + 2) % 4)

    def tok_pair(s, j):
        of = y_of[s] * 2 + c
        src = tokb.at[0, pl.ds(PIECE * j, PIECE), cols(of)]
        push(src, piece(j, of), rt.at[s, j], pair, S_TOK)

    def tok_arrived(s, j):
        ref = piece(j, y_of[s] * 2 + c)
        arrive(ref, rt.at[s, j])
        if s == 0:
            push(ref, ref, rt.at[1, j], yup, S_TOK)
            push(ref, ref, rt.at[2, j], ydown, S_TOK)
        if s == 1 and j < RELAYED:
            push(ref, ref, rt.at[3, j], yup, S_TOK)
        if s == 2 and RELAYED <= j < 2 * RELAYED:
            push(ref, ref, rt.at[3, j], ydown, S_TOK)

    def quarter(b, head_of):
        return tokb.at[1, pl.ds(128 * b, 128), cols(head_of)]

    def to_sibling(s, b):
        ref = quarter(b, y_of[s] * 2 + c)
        push(ref, ref, rs.at[0], sib, S_TOK)

    def from_sibling(s, b):
        if counted("sibling", 16):
            arrive(tokb.at[1, pl.ds(0, 256), :], rs.at[0])

    def tables(t):
        rank = dp if t == 0 else xp * 8 + z
        row = lax.broadcasted_iota(jnp.int32, (ROWS, HD), 0)
        lane = lax.broadcasted_iota(jnp.int32, (ROWS, HD), 1)
        start = jnp.zeros((ROWS, HD), jnp.int32)
        end = 0
        for d in range(16):
            n = dl[d, rank]
            end = end + n
            start = start + jnp.where(row >= end, n, 0)
        angle = (row - start).astype(F32) * freq[...]
        cosb[t] = jnp.cos(angle)
        s = jnp.sin(angle)
        sinb[t] = jnp.where(lane < 64, -s, s)
        for j in range(4):
            col = lane + 128 * j
            bias[t, :, 128 * j:128 * j + 128] = jnp.where(
                (col >= start) & (col <= row), 0.0, -1e30)

    def norm_rope(u, gain, t):
        ms = jnp.mean(u * u, axis=-1, keepdims=True)
        n = u * lax.rsqrt(ms + EPS) * gain
        return (n * cosb[t] + pltpu.roll(n, 64, 1) * sinb[t]).astype(BF16)

    def lhs(t, ps):
        parts = []
        for p in ps:
            zz = (z + 8 + (-1 if p % 2 else 1) * ((p + 1) // 2)) % 8
            for xx in (x, xn, xp, 3 - xn):
                f = pl.multiple_of((xx * 8 + zz) * 128, 128)
                parts.append(tokb[t, :, pl.ds(f, 128)])
        return jnp.concatenate(parts, axis=1)

    def dots(t, ps, g):
        def go():
            width = 128 if g == 0 else 256
            b = group(g)[pl.ds(4 * ps[0], 4 * len(ps))].reshape(512 * len(ps), width)
            total = kvacc.at[t] if g == 0 else acc.at[t, g - 1]
            new = jnp.dot(lhs(t, ps), b, preferred_element_type=F32)
            total[...] = new if ps[0] == 0 else total[...] + new
        guarded(g, go)

    def kv_finish(t):
        @pl.when(worker & (is_v == 0))
        def _():
            kvst[t] = norm_rope(kvacc[t], kg[...], t)

        @pl.when(worker & (is_v == 1))
        def _():
            kvst[t] = kvacc[t].astype(BF16)

    def kv_send(t):
        def send_to(xx, tt, sid):
            push(kvst.at[t], kvin.at[is_v, tt], rkv.at[tt], dev(xx, z, kv_to, c), sid)

        pl.when(worker)(lambda: send_to(xp, 1 - t, S_KEYS))
        pl.when(worker & (kv_to != y))(lambda: send_to(x, t, S_BEYOND))

        @pl.when(worker & (kv_to == y))
        def _():
            pltpu.make_async_copy(kvst.at[t], kvin.at[is_v, t], rkv.at[t]).start()

    first_core = c == y % 2

    def kv_arrived(t):
        arrive(kvst, rkv.at[t])

        @pl.when(first_core)
        def _():
            push(kvin.at[:, t], kvin.at[:, t], rkv.at[t], sib, S_SHARE)

    scale = HD ** -0.5 * math.log2(math.e)

    def attend(t, g, hh):
        q = norm_rope(acc[t, g - 1, :, 128 * hh:128 * hh + 128], qg[...], t)
        for i in (0, 1):
            m = 256 * (i + 1)
            s = lax.dot_general(q[256 * i:m], kvin[0, t, :m], (((1,), (1,)), ((), ())),
                                preferred_element_type=F32)
            e = jnp.exp2(s * scale + bias[t, 256 * i:m, :m]).astype(BF16)
            v = jnp.concatenate([kvin[1, t, :m], jnp.ones((m, HD), BF16)], axis=1)
            o = jnp.dot(e, v, preferred_element_type=F32)
            at = (g - 1) * 256 + 128 * hh
            ost[t, 256 * i:m, at:at + 128] = (o[:, :HD] / o[:, HD:]).astype(BF16)

    def emit(t, g, hh):
        at = (g - 1) * 256 + hh * 128
        here = ost.at[t, :, pl.ds(at, 128)]
        there = out.at[:, pl.ds(pl.multiple_of(side * 512 + at, 128), 128)]
        if t == 1:
            push(here, there, rout.at[0], pair, S_OUT)
        else:
            pltpu.make_async_copy(here, there, loc.at[3]).start()

    def weights(g, q, xi):
        def go():
            wait_w(g, q, xi)
            if 0 < q < 7 and xi != FAR:
                d = (q + 1) % 2
                src = slot(g, q, xi) if q < 5 else half(g, q, xi, d)
                on = q + 2
                push(src, slot(g, on, xi), rsem_of(g, on, xi), (up, down)[d], g)
            if xi == PAIR:
                cross(g, q)
        guarded(g, go)

    load_kv.wait()
    arrive(wbuf.at[0, pl.ds(0, 4)], loc.at[2])
    once = set()

    def first(name):
        new = name not in once
        once.add(name)
        return new

    for what, *a in ORDER:
        if what == "tables" and first("small"):
            for copy in small:
                copy.wait()
        if what in ("dots", "tokp") and first("tok"):
            load_tok.wait()
        if what == "near":
            start_near(*a)
        elif what == "pair":
            start_pair(*a)
        elif what == "tokp":
            tok_pair(0, *a)
        elif what == "tokp2":
            tok_pair(3, *a)
        elif what == "src":
            ring_start(*a)
        elif what == "w":
            weights(*a)
        elif what == "t":
            tok_arrived(*a)
        elif what == "sib":
            to_sibling(*a)
        elif what == "s":
            from_sibling(*a)
        elif what == "tables":
            tables(*a)
        elif what == "dots":
            dots(*a)
        elif what == "kv":
            kv_finish(*a)
            kv_send(*a)
        elif what == "kvin":
            kv_arrived(*a)
        elif what == "att":
            attend(*a)
            emit(*a)

    for g in (1, 2):
        arrive(group(g).at[pl.ds(0, 31)], send.at[g])
    arrive(tokb.at[1], send.at[S_TOK])
    arrive(ost.at[0], send.at[S_OUT])

    @pl.when(worker)
    def _():
        arrive(kvbuf.at[pl.ds(0, 30)], send.at[S_KV])
        arrive(kvst, send.at[S_KEYS])

    @pl.when(first_core)
    def _():
        arrive(kvin, send.at[S_SHARE])

    @pl.when(worker & (kv_to != y))
    def _():
        arrive(kvst, send.at[S_BEYOND])

    @pl.when(jnp.logical_not(worker))
    def _():
        arrive(kvbuf.at[0], send.at[S_HELP])

    arrive(ost.at[0], loc.at[3])
    arrive(ost.at[1], rout.at[0])


def shards(tokens, q_weight, kv_weight, q_gain, k_gain, doc_lengths):
    half = np.exp(np.arange(64) * (-2.0 * math.log(THETA) / HD)).astype(np.float32)
    freq = jnp.asarray(np.concatenate([half, half])[None, :])
    any_ = pl.BlockSpec(memory_space=pl.ANY)
    dma = pltpu.SemaphoreType.DMA
    return pl.pallas_call(
        kernel,
        out_shape=jax.ShapeDtypeStruct((ROWS, 1024), BF16),
        in_specs=[any_] * 7,
        out_specs=any_,
        scratch_shapes=[
            pltpu.VMEM((2, ROWS, FEAT), BF16),
            pltpu.VMEM((2, 32, 128, 256), BF16),
            pltpu.VMEM((32, 128, 128), BF16),
            pltpu.VMEM((2, 128, 256), BF16),
            pltpu.VMEM((2, 2, ROWS, 256), F32),
            pltpu.VMEM((2, ROWS, 128), F32),
            pltpu.VMEM((2, ROWS, 128), BF16),
            pltpu.VMEM((2, 2, ROWS, 128), BF16),
            pltpu.VMEM((2, ROWS, HD), F32),
            pltpu.VMEM((2, ROWS, HD), F32),
            pltpu.VMEM((2, ROWS, ROWS), F32),
            pltpu.VMEM((2, ROWS, 512), BF16),
            pltpu.VMEM((1, HD), F32),
            pltpu.VMEM((1, HD), F32),
            pltpu.VMEM((1, HD), F32),
            pltpu.SMEM((16, 32), jnp.int32),
            dma((9,)),
            dma((3, 27)),
            dma((4, 8)),
            dma((1,)),
            dma((2,)),
            dma((1,)),
            dma((8,)),
        ],
        compiler_params=pltpu.CompilerParams(
            collective_id=0, has_side_effects=True, vmem_limit_bytes=60 * 2**20),
        cost_estimate=pl.CostEstimate(
            flops=6_000_000_000, bytes_accessed=12 * 2**20, transcendentals=2**21),
    )(tokens, q_weight, kv_weight, q_gain[None, :], k_gain[None, :], freq, doc_lengths.T)


def solution(mesh):
    placed = (P("dp", None), P("dp", "head"), P("dp", "head"), P(), P(), P())
    return jax.shard_map(
        shards, mesh=mesh, in_specs=placed, out_specs=P("dp", "head"), check_vma=False
    )
```

time: 222 us -> 65.9 us (0.30)
  waiting for transfers between devices: 168 us -> 0 us
  Pallas kernels: 0 us -> 63.5 us
  matrix products: 17.3 us -> 0 us
  blocking collectives: 14.7 us -> 0 us
  between operations: 13.5 us -> 0.01 us
  other arithmetic: 6.22 us -> 0 us
    all_gather x2 -> x0, waiting for transfers between devices: 167 us -> none  [the longest x1 96.7 us: shards(): q_sum = add_rows(lax.all_gather(q_weight, 'dp', axis=0, tiled=True))]
    pallas_call x0 -> x1, Pallas kernels: none -> 63.5 us  [shards(): pl.pallas_call(kernel, out_shape=jax.ShapeDtypeStruct((ROWS, 1024), BF16)...]
    dot_general x4 -> x0, matrix products: 17.3 us -> none  [the longest x2 12.3 us: add_rows(): return jnp.dot(tokens, shard_rows, preferred_element_type=jnp.float32)]
    all_gather x1 -> x0, blocking collectives: 14.7 us -> none  [shards(): kv_all = lax.all_gather(kv_weight, 'head', axis=1, tiled=True)]
  transfers between devices with their start and end apart: 2 -> 0, of which waited for: 2 -> 0; matrix products, arithmetic and copies ran while one was open for 4% -> 0% of each run, Pallas kernels for 0% -> 0%
where the time goes in v2:
time: 65.9 us; the launch traced here: 65.8 us
  Pallas kernels  63.5 us (96%)
  local copies, waits for them, and re-layouts  2.26 us (3%)
    pallas_call x1, Pallas kernels, shards(): pl.pallas_call(kernel, out_shape=jax.ShapeDtypeStruct((ROWS, 1024), BF16)...  63.5 us
    unnamed x1, local copies, waits for them, and re-layouts  2.26 us

profile of v2, /device:TPU:1, one launch (start us, length us, event | category | flops | bytes accessed | tf_op | source)
XLA Modules:
  0.0 65.8 jit_solution(11008779867087980278)
XLA Ops:
  0.0 63.5 %shard_map.73 = bf16[512,1024]{1,0:T(8,128)(2,1)} custom-call(bf16[512,4096]{1,0:T(8,128)(2,1)} %tok.1, bf16[128,1024]{1,0:T(8,128)(2,1)} %w.1, bf16[128,128]{1,0:T(8,128)(2,1)} %kvw.1, f32[1,128]{1,0:T(1,128)} %bitcast.4, f32[1,128]{1,0:T(1,128)} %bitcast.5, f32[1,128]{1,0:T(1,128)} %constant.2.clone.freq_in, s32[16,32]{1,0:T(8,128)} %bitcast.3), custom_call_target="tpu_custom_call" | custom-call | flops 6000000000 | bytes 12582912 | tf_op jit(solution)/shard_map/pallas_call | solution.py:408
  63.5 2.3 %copy.9 = bf16[512,1024]{1,0:T(8,128)(2,1)} copy(bf16[512,1024]{1,0:T(8,128)(2,1)} %shard_map.73) | data formatting | bytes 2097152

commit v3 on v2

--- a/solution.py
+++ b/solution.py
@@ -17,7 +17,7 @@
 MESH = pl.DeviceIdType.MESH
 F32 = jnp.float32
 BF16 = jnp.bfloat16
-S_KV, S_HELP, S_TOK, S_KEYS, S_BEYOND, S_OUT, S_SHARE = 0, 3, 4, 5, 6, 7, 8
+S_KV, S_HELP, S_TOK, S_KEYS, S_BEYOND, S_QUERY = 0, 3, 4, 5, 6, 7
 GROUPS = (0, 1, 2)
 OWN, NEAR, PAIR, FAR = 0, 1, 2, 3
 
@@ -26,43 +26,43 @@
 RELAYED = 2
 
 ORDER = (
-    ("pair",0), ("pair",1), ("tokp",0), ("tokp",1), ("pair",2), ("tokp",2), ("tokp",3), ("tokp",4),
-    ("tokp",5), ("tokp",6), ("tokp",7), ("tokp2",4), ("tokp2",5), ("tokp2",6), ("tokp2",7), ("near",0),
-    ("near",1), ("near",2), ("src",0,0), ("tables",0), ("src",1,0), ("src",2,0), ("tables",1), ("w",0,0,2),
-    ("src",0,2), ("w",0,0,1), ("src",0,1), ("w",0,1,0), ("w",0,2,0), ("w",1,0,2), ("src",1,2), ("w",1,0,1),
-    ("w",1,1,0), ("w",1,2,0), ("t",0,0), ("w",2,0,1), ("w",2,1,0), ("w",2,2,0), ("w",0,0,3), ("w",0,1,2),
-    ("w",0,2,2), ("w",0,1,1), ("w",0,2,1), ("w",0,3,0), ("w",0,4,0), ("t",0,1), ("sib",0,0), ("w",1,0,3),
-    ("w",1,1,2), ("w",1,2,2), ("s",0,0), ("w",2,0,2), ("w",0,1,3), ("w",0,2,3), ("t",1,0), ("t",2,0),
-    ("w",1,3,0), ("w",1,4,0), ("t",0,2), ("t",1,1), ("sib",1,0), ("t",2,1), ("sib",2,0), ("w",2,3,0),
-    ("w",2,4,0), ("t",0,3), ("sib",0,1), ("w",0,3,2), ("w",0,4,2), ("w",0,3,1), ("w",0,4,1), ("w",1,1,3),
-    ("w",0,5,0), ("w",0,6,0), ("s",1,0), ("s",2,0), ("t",0,4), ("s",0,1), ("t",3,0), ("w",1,2,3),
-    ("src",1,1), ("w",1,3,2), ("w",1,4,2), ("t",2,2), ("t",0,5), ("sib",0,2), ("t",1,2), ("w",2,0,3),
-    ("w",1,5,0), ("w",1,6,0), ("t",2,3), ("sib",2,1), ("w",0,3,3), ("w",0,4,3), ("dots",0,(0,1,2,3,4),0),
-    ("s",0,2), ("t",0,6), ("t",3,1), ("sib",3,0), ("w",2,5,0), ("w",2,6,0), ("s",2,1), ("t",2,4),
-    ("w",0,5,2), ("w",0,6,2), ("t",0,7), ("sib",0,3), ("w",0,5,1), ("w",0,6,1), ("w",0,7,0), ("w",0,8,0),
-    ("w",1,3,3), ("t",1,3), ("sib",1,1), ("s",3,0), ("t",3,2), ("src",2,2), ("s",0,3), ("t",3,4),
-    ("w",1,1,1), ("w",1,2,1), ("dots",0,(0,1,2),1), ("w",1,4,3), ("s",1,1), ("t",1,4), ("t",2,5),
-    ("sib",2,2), ("w",0,5,3), ("w",0,6,3), ("dots",0,(5,6),0), ("t",3,5), ("sib",3,2), ("w",1,5,2),
-    ("w",1,6,2), ("t",1,5), ("sib",1,2), ("s",2,2), ("t",3,3), ("sib",3,1), ("w",1,7,0), ("w",1,8,0),
-    ("t",3,6), ("w",2,7,0), ("w",2,8,0), ("src",2,1), ("s",3,2), ("w",0,7,2), ("w",0,8,2), ("t",1,6),
-    ("w",0,7,1), ("w",0,8,1), ("s",1,2), ("t",2,6), ("s",3,1), ("t",3,7), ("sib",3,3), ("t",1,7),
-    ("sib",1,3), ("w",2,1,2), ("w",2,2,2), ("t",2,7), ("sib",2,3), ("w",1,5,3), ("s",3,3), ("s",1,3),
-    ("w",1,3,1), ("w",1,4,1), ("dots",0,(3,4),1), ("s",2,3), ("dots",1,(0,1,2,3,4,5,6),0), ("w",1,6,3),
-    ("w",1,7,2), ("w",1,8,2), ("w",0,7,3), ("w",0,8,3), ("dots",1,(7,),0), ("kv",1), ("w",2,1,1),
-    ("w",2,2,1), ("w",2,1,3), ("dots",0,(7,),0), ("kv",0), ("dots",1,(0,1,2,3,4),1), ("w",2,3,2),
-    ("w",2,4,2), ("w",2,2,3), ("dots",0,(0,1,2),2), ("w",1,7,3), ("w",1,5,1), ("w",1,6,1),
-    ("dots",1,(5,6),1), ("dots",0,(5,6),1), ("w",1,8,3), ("w",2,3,1), ("w",2,4,1), ("w",2,5,2), ("w",2,3,3),
-    ("w",2,6,2), ("w",1,7,1), ("w",1,8,1), ("dots",1,(7,),1), ("dots",0,(7,),1), ("kvin",1), ("att",1,1,0),
-    ("w",2,4,3), ("att",1,1,1), ("w",2,5,1), ("w",2,6,1), ("dots",1,(0,1,2,3,4),2), ("kvin",0), ("w",2,7,2),
-    ("w",2,8,2), ("dots",0,(3,4),2), ("w",2,5,3), ("att",0,1,0), ("att",0,1,1), ("w",2,6,3),
-    ("dots",1,(5,6),2), ("w",2,7,1), ("w",2,8,1), ("dots",0,(5,6),2), ("w",2,7,3), ("w",2,8,3),
-    ("dots",1,(7,),2), ("att",1,2,0), ("att",1,2,1), ("dots",0,(7,),2), ("att",0,2,0), ("att",0,2,1),
+    ("pair",0), ("near",0), ("pair",1), ("tokp",0), ("src",2,0), ("w",2,8,0), ("tables",0), ("near",2),
+    ("w",0,0,3), ("src",1,0), ("near",1), ("s",3,0), ("src",0,0), ("tokp",1), ("tokp2",7), ("w",2,2,0),
+    ("tokp",3), ("tokp",2), ("w",2,7,0), ("w",0,0,2), ("s",2,3), ("tokp",4), ("w",1,0,2), ("w",0,0,1),
+    ("tokp",6), ("src",0,2), ("pair",2), ("s",2,2), ("src",1,2), ("src",0,1), ("w",2,1,0), ("t",0,0),
+    ("tables",1), ("w",0,2,0), ("w",0,1,0), ("w",1,1,0), ("w",1,2,0), ("tokp",5), ("w",2,1,3), ("w",2,0,1),
+    ("tokp2",4), ("w",0,7,3), ("t",0,1), ("w",0,1,2), ("tokp2",5), ("src",2,1), ("w",0,2,2), ("t",2,0),
+    ("w",1,0,1), ("w",0,2,1), ("w",0,1,1), ("t",0,2), ("sib",0,0), ("t",1,0), ("tokp",7), ("t",0,3),
+    ("w",1,1,2), ("w",0,5,3), ("w",1,2,2), ("src",1,1), ("w",0,3,2), ("w",0,3,0), ("w",0,4,0), ("t",2,1),
+    ("w",2,4,0), ("w",0,4,2), ("w",1,2,3), ("t",0,4), ("w",2,0,3), ("tokp2",6), ("w",1,4,3), ("w",1,4,0),
+    ("w",0,4,1), ("w",1,1,3), ("w",1,3,0), ("w",0,3,1), ("s",2,1), ("t",2,2), ("w",1,5,3), ("w",1,4,2),
+    ("s",1,0), ("t",0,6), ("w",1,0,3), ("w",0,2,3), ("t",1,1), ("w",0,4,3), ("w",1,3,2), ("s",0,3),
+    ("s",1,1), ("w",2,0,2), ("w",1,7,3), ("src",2,2), ("t",0,5), ("w",0,5,0), ("t",3,4), ("t",1,2),
+    ("w",0,6,2), ("t",1,3), ("w",0,7,0), ("w",0,5,2), ("w",2,6,0), ("sib",0,2), ("t",2,3), ("w",2,3,0),
+    ("w",0,3,3), ("w",0,1,3), ("w",1,7,0), ("t",2,4), ("w",1,2,1), ("s",1,2), ("sib",2,0), ("s",3,3),
+    ("sib",2,1), ("w",1,1,1), ("dots",0,(0,1,2,3,4),0), ("t",0,7), ("w",1,5,2), ("s",3,1), ("t",3,7),
+    ("sib",0,3), ("w",0,5,1), ("w",0,8,1), ("t",3,0), ("dots",0,(0,1,2),1), ("t",1,4), ("w",0,6,0),
+    ("t",3,1), ("sib",1,0), ("w",1,6,2), ("sib",1,1), ("t",2,5), ("s",2,0), ("s",0,2), ("w",0,8,0),
+    ("w",0,6,1), ("w",2,3,3), ("s",0,0), ("sib",3,0), ("sib",0,1), ("w",0,7,2), ("t",3,5), ("s",3,2),
+    ("t",1,5), ("w",0,8,2), ("t",3,6), ("w",0,6,3), ("sib",3,2), ("w",2,7,1), ("w",2,1,2), ("t",3,3),
+    ("w",2,1,1), ("w",2,2,2), ("w",1,3,3), ("w",2,2,1), ("dots",0,(5,6),0), ("sib",2,2), ("t",1,6),
+    ("t",3,2), ("sib",3,1), ("sib",1,2), ("sib",3,3), ("t",2,6), ("t",1,7), ("sib",1,3), ("t",2,7),
+    ("w",2,5,3), ("s",0,1), ("w",1,4,1), ("w",1,3,1), ("sib",2,3), ("w",1,7,2), ("w",1,8,2), ("s",1,3),
+    ("dots",1,(0,1,2,3,4,5,6),0), ("w",2,4,2), ("w",0,8,3), ("w",2,3,2), ("w",0,7,1), ("dots",1,(7,),0),
+    ("w",1,6,0), ("kv",1), ("w",1,6,3), ("w",2,3,1), ("w",1,8,0), ("w",2,4,1), ("dots",1,(0,1,2,3,4),1),
+    ("w",1,5,0), ("w",1,6,1), ("dots",0,(7,),0), ("w",1,5,1), ("kv",0), ("w",2,2,3), ("w",2,5,2),
+    ("w",2,6,2), ("dots",1,(5,6),1), ("w",2,5,1), ("w",1,7,1), ("dots",0,(0,1,2),2), ("w",2,5,0),
+    ("dots",0,(3,4),1), ("w",1,8,3), ("w",1,8,1), ("dots",1,(7,),1), ("q",1), ("w",2,6,1),
+    ("dots",0,(5,6),1), ("w",2,8,2), ("dots",0,(7,),1), ("w",2,4,3), ("w",2,7,2), ("dots",1,(0,1,2,3,4),2),
+    ("w",2,6,3), ("dots",0,(3,4),2), ("w",2,8,3), ("dots",1,(5,6),2), ("w",2,7,3), ("w",2,8,1),
+    ("dots",1,(7,),2), ("q",2), ("dots",0,(5,6),2), ("qin",1,0), ("dots",0,(7,),2), ("kvin",), ("qin",1,1),
+    ("att",1,1), ("att",0,2), ("att",0,1), ("qin",2,0), ("att",1,2,0), ("qin",2,1), ("att",1,2,1),
 )
 
 
 def kernel(tok, w, kvw, qg_in, kg_in, freq_in, dl_in, out,
-           tokb, wbuf, kvbuf, stage, acc, kvacc, kvst, kvin, cosb, sinb, bias, ost, qg, kg, freq, dl,
-           send, rw, rt, rs, rkv, rout, loc):
+           tokb, wbuf, kvbuf, stage, acc, kvacc, kvst, kvin, cosb, sinb, bias, ost, qst, qin, qg, kg, freq, dl,
+           send, rw, rt, rs, rkv, rq, loc):
     dp = lax.axis_index("dp")
     hd = lax.axis_index("head")
     x, z = dp // 8, dp % 8
@@ -106,11 +106,11 @@
     kv_self = worker & (kv_to == y)
     for v in (0, 1):
         src_y = 2 * v + y // 2
-        @pl.when((c == src_side) & jnp.logical_not(kv_self & (is_v == v)))
+        @pl.when(jnp.logical_not(kv_self & (is_v == v)))
         def _():
             pl.semaphore_signal(
                 barrier, inc=1, device_id=dev(src_x, z, src_y, src_side), device_id_type=MESH)
-    extra = jnp.where(worker, jnp.where(kv_to == y, 1, 2), 0)
+    extra = jnp.where(worker, jnp.where(kv_to == y, 3, 4), 0)
     pl.semaphore_wait(barrier, 7 + extra)
 
     def push(src, dst, rsem, to, sid):
@@ -236,13 +236,19 @@
         cosb[t] = jnp.cos(angle)
         s = jnp.sin(angle)
         sinb[t] = jnp.where(lane < 64, -s, s)
-        for j in range(4):
+        for j in range(4 if t == 0 else 0):
             col = lane + 128 * j
-            bias[t, :, 128 * j:128 * j + 128] = jnp.where(
-                (col >= start) & (col <= row), 0.0, -1e30)
-
-    def norm_rope(u, gain, t):
-        ms = jnp.mean(u * u, axis=-1, keepdims=True)
+            bias[:, 128 * j:128 * j + 128] = jnp.where((col >= start) & (col <= row), 0.0, -1e30)
+
+    def norm_rope(u, gain, t, by_matrix_unit=False):
+        square = u * u
+        if by_matrix_unit:
+            high = square.astype(BF16)
+            low = (square - high.astype(F32)).astype(BF16)
+            ms = jnp.dot(jnp.concatenate([high, low], axis=1), jnp.full((2 * HD, HD), 1.0 / HD, BF16),
+                         preferred_element_type=F32)
+        else:
+            ms = jnp.mean(square, axis=-1, keepdims=True)
         n = u * lax.rsqrt(ms + EPS) * gain
         return (n * cosb[t] + pltpu.roll(n, 64, 1) * sinb[t]).astype(BF16)
 
@@ -274,47 +280,57 @@
             kvst[t] = kvacc[t].astype(BF16)
 
     def kv_send(t):
-        def send_to(xx, tt, sid):
-            push(kvst.at[t], kvin.at[is_v, tt], rkv.at[tt], dev(xx, z, kv_to, c), sid)
-
-        pl.when(worker)(lambda: send_to(xp, 1 - t, S_KEYS))
-        pl.when(worker & (kv_to != y))(lambda: send_to(x, t, S_BEYOND))
+        def send_to(xx, core, sid):
+            push(kvst.at[t], kvin.at[is_v], rkv.at[0], dev(xx, z, kv_to, core), sid)
+
+        @pl.when(worker)
+        def _():
+            if t == 1:
+                send_to(xp, c, S_KEYS)
+                send_to(xp, 1 - c, S_KEYS)
+            else:
+                send_to(x, 1 - c, S_KEYS)
+
+        if t == 1:
+            return
+        pl.when(worker & (kv_to != y))(lambda: send_to(x, c, S_BEYOND))
 
         @pl.when(worker & (kv_to == y))
         def _():
-            pltpu.make_async_copy(kvst.at[t], kvin.at[is_v, t], rkv.at[t]).start()
-
-    first_core = c == y % 2
-
-    def kv_arrived(t):
-        arrive(kvst, rkv.at[t])
-
-        @pl.when(first_core)
-        def _():
-            push(kvin.at[:, t], kvin.at[:, t], rkv.at[t], sib, S_SHARE)
+            pltpu.make_async_copy(kvst.at[t], kvin.at[is_v], rkv.at[0]).start()
+
+    def kv_arrived():
+        arrive(kvin, rkv.at[0])
 
     scale = HD ** -0.5 * math.log2(math.e)
 
-    def attend(t, g, hh):
-        q = norm_rope(acc[t, g - 1, :, 128 * hh:128 * hh + 128], qg[...], t)
+    def query(t, g, hh):
+        u = acc[t, g - 1, :, 128 * hh:128 * hh + 128]
+        return norm_rope(u, qg[...], t, by_matrix_unit=t == 0)
+
+    def send_queries(g):
+        for hh in (0, 1):
+            n = 2 * (g - 1) + hh
+            qst[n] = query(1, g, hh)
+            push(qst.at[n], qin.at[n], rq.at[n], pair, S_QUERY)
+
+    def attend(of, g, hh):
+        n = 2 * (g - 1) + hh
+        q = query(0, g, hh) if of == 0 else qin[n]
         for i in (0, 1):
             m = 256 * (i + 1)
-            s = lax.dot_general(q[256 * i:m], kvin[0, t, :m], (((1,), (1,)), ((), ())),
+            s = lax.dot_general(q[256 * i:m], kvin[0, :m], (((1,), (1,)), ((), ())),
                                 preferred_element_type=F32)
-            e = jnp.exp2(s * scale + bias[t, 256 * i:m, :m]).astype(BF16)
-            v = jnp.concatenate([kvin[1, t, :m], jnp.ones((m, HD), BF16)], axis=1)
+            e = jnp.exp2(s * scale + bias[256 * i:m, :m]).astype(BF16)
+            v = jnp.concatenate([kvin[1, :m], jnp.ones((m, HD), BF16)], axis=1)
             o = jnp.dot(e, v, preferred_element_type=F32)
-            at = (g - 1) * 256 + 128 * hh
-            ost[t, 256 * i:m, at:at + 128] = (o[:, :HD] / o[:, HD:]).astype(BF16)
-
-    def emit(t, g, hh):
-        at = (g - 1) * 256 + hh * 128
-        here = ost.at[t, :, pl.ds(at, 128)]
-        there = out.at[:, pl.ds(pl.multiple_of(side * 512 + at, 128), 128)]
-        if t == 1:
-            push(here, there, rout.at[0], pair, S_OUT)
-        else:
-            pltpu.make_async_copy(here, there, loc.at[3]).start()
+            ost[of, 256 * i:m, 128 * n:128 * n + 128] = (o[:, :HD] / o[:, HD:]).astype(BF16)
+
+    def emit(of, g, hh):
+        at = 128 * (2 * (g - 1) + hh)
+        first_col = (side if of == 0 else 1 - side) * 512 + at
+        pltpu.make_async_copy(ost.at[of, :, pl.ds(at, 128)],
+                              out.at[:, pl.ds(pl.multiple_of(first_col, 128), 128)], loc.at[3]).start()
 
     def weights(g, q, xi):
         def go():
@@ -341,7 +357,7 @@
         if what == "tables" and first("small"):
             for copy in small:
                 copy.wait()
-        if what in ("dots", "tokp") and first("tok"):
+        if what in ("dots", "tokp", "tokp2") and first("tok"):
             load_tok.wait()
         if what == "near":
             start_near(*a)
@@ -369,35 +385,38 @@
             kv_finish(*a)
             kv_send(*a)
         elif what == "kvin":
-            kv_arrived(*a)
+            kv_arrived()
+        elif what == "q":
+            send_queries(*a)
+        elif what == "qin":
+            n = 2 * (a[0] - 1) + a[1]
+            arrive(qin.at[n], rq.at[n])
         elif what == "att":
-            attend(*a)
-            emit(*a)
+            heads = (0, 1) if len(a) == 2 else a[2:]
+            for hh in heads:
+                attend(a[0], a[1], hh)
+            for hh in heads:
+                emit(a[0], a[1], hh)
 
     for g in (1, 2):
         arrive(group(g).at[pl.ds(0, 31)], send.at[g])
     arrive(tokb.at[1], send.at[S_TOK])
-    arrive(ost.at[0], send.at[S_OUT])
+    arrive(qst, send.at[S_QUERY])
 
     @pl.when(worker)
     def _():
         arrive(kvbuf.at[pl.ds(0, 30)], send.at[S_KV])
-        arrive(kvst, send.at[S_KEYS])
-
-    @pl.when(first_core)
-    def _():
-        arrive(kvin, send.at[S_SHARE])
+        arrive(wbuf.at[0, pl.ds(0, 6)], send.at[S_KEYS])
 
     @pl.when(worker & (kv_to != y))
     def _():
-        arrive(kvst, send.at[S_BEYOND])
+        arrive(kvst.at[0], send.at[S_BEYOND])
 
     @pl.when(jnp.logical_not(worker))
     def _():
         arrive(kvbuf.at[0], send.at[S_HELP])
 
-    arrive(ost.at[0], loc.at[3])
-    arrive(ost.at[1], rout.at[0])
+    arrive(ost, loc.at[3])
 
 
 def shards(tokens, q_weight, kv_weight, q_gain, k_gain, doc_lengths):
@@ -418,21 +437,23 @@
             pltpu.VMEM((2, 2, ROWS, 256), F32),
             pltpu.VMEM((2, ROWS, 128), F32),
             pltpu.VMEM((2, ROWS, 128), BF16),
-            pltpu.VMEM((2, 2, ROWS, 128), BF16),
+            pltpu.VMEM((2, ROWS, 128), BF16),
             pltpu.VMEM((2, ROWS, HD), F32),
             pltpu.VMEM((2, ROWS, HD), F32),
-            pltpu.VMEM((2, ROWS, ROWS), F32),
+            pltpu.VMEM((ROWS, ROWS), F32),
             pltpu.VMEM((2, ROWS, 512), BF16),
+            pltpu.VMEM((4, ROWS, HD), BF16),
+            pltpu.VMEM((4, ROWS, HD), BF16),
             pltpu.VMEM((1, HD), F32),
             pltpu.VMEM((1, HD), F32),
             pltpu.VMEM((1, HD), F32),
             pltpu.SMEM((16, 32), jnp.int32),
-            dma((9,)),
+            dma((8,)),
             dma((3, 27)),
             dma((4, 8)),
             dma((1,)),
-            dma((2,)),
             dma((1,)),
+            dma((4,)),
             dma((8,)),
         ],
         compiler_params=pltpu.CompilerParams(

time: 65.9 us -> 63.2 us (0.959)
  Pallas kernels: 63.5 us -> 60.8 us
    pallas_call x1, Pallas kernels: 63.5 us -> 60.8 us  [shards(): pl.pallas_call(kernel, out_shape=jax.ShapeDtypeStruct((ROWS, 1024), BF16)...]
where the time goes in v3:
time: 63.2 us; the launch traced here: 63.1 us
  Pallas kernels  60.8 us (96%)
  local copies, waits for them, and re-layouts  2.26 us (4%)
    pallas_call x1, Pallas kernels, shards(): pl.pallas_call(kernel, out_shape=jax.ShapeDtypeStruct((ROWS, 1024), BF16)...  60.8 us
    unnamed x1, local copies, waits for them, and re-layouts  2.26 us

profile of v3, /device:TPU:1, one launch (start us, length us, event | category | flops | bytes accessed | tf_op | source)
XLA Modules:
  0.0 63.1 jit_solution(11735428702836784067)
XLA Ops:
  0.0 60.8 %shard_map.73 = bf16[512,1024]{1,0:T(8,128)(2,1)} custom-call(bf16[512,4096]{1,0:T(8,128)(2,1)} %tok.1, bf16[128,1024]{1,0:T(8,128)(2,1)} %w.1, bf16[128,128]{1,0:T(8,128)(2,1)} %kvw.1, f32[1,128]{1,0:T(1,128)} %bitcast.4, f32[1,128]{1,0:T(1,128)} %bitcast.5, f32[1,128]{1,0:T(1,128)} %constant.2.clone.freq_in, s32[16,32]{1,0:T(8,128)} %bitcast.3), custom_call_target="tpu_custom_call" | custom-call | flops 6000000000 | bytes 12582912 | tf_op jit(solution)/shard_map/pallas_call | solution.py:427
  60.8 2.3 %copy.9 = bf16[512,1024]{1,0:T(8,128)(2,1)} copy(bf16[512,1024]{1,0:T(8,128)(2,1)} %shard_map.73) | data formatting | bytes 2097152

commit v4 on v3

--- a/solution.py
+++ b/solution.py
@@ -26,37 +26,37 @@
 RELAYED = 2
 
 ORDER = (
-    ("pair",0), ("near",0), ("pair",1), ("tokp",0), ("src",2,0), ("w",2,8,0), ("tables",0), ("near",2),
-    ("w",0,0,3), ("src",1,0), ("near",1), ("s",3,0), ("src",0,0), ("tokp",1), ("tokp2",7), ("w",2,2,0),
-    ("tokp",3), ("tokp",2), ("w",2,7,0), ("w",0,0,2), ("s",2,3), ("tokp",4), ("w",1,0,2), ("w",0,0,1),
-    ("tokp",6), ("src",0,2), ("pair",2), ("s",2,2), ("src",1,2), ("src",0,1), ("w",2,1,0), ("t",0,0),
-    ("tables",1), ("w",0,2,0), ("w",0,1,0), ("w",1,1,0), ("w",1,2,0), ("tokp",5), ("w",2,1,3), ("w",2,0,1),
-    ("tokp2",4), ("w",0,7,3), ("t",0,1), ("w",0,1,2), ("tokp2",5), ("src",2,1), ("w",0,2,2), ("t",2,0),
-    ("w",1,0,1), ("w",0,2,1), ("w",0,1,1), ("t",0,2), ("sib",0,0), ("t",1,0), ("tokp",7), ("t",0,3),
-    ("w",1,1,2), ("w",0,5,3), ("w",1,2,2), ("src",1,1), ("w",0,3,2), ("w",0,3,0), ("w",0,4,0), ("t",2,1),
-    ("w",2,4,0), ("w",0,4,2), ("w",1,2,3), ("t",0,4), ("w",2,0,3), ("tokp2",6), ("w",1,4,3), ("w",1,4,0),
-    ("w",0,4,1), ("w",1,1,3), ("w",1,3,0), ("w",0,3,1), ("s",2,1), ("t",2,2), ("w",1,5,3), ("w",1,4,2),
-    ("s",1,0), ("t",0,6), ("w",1,0,3), ("w",0,2,3), ("t",1,1), ("w",0,4,3), ("w",1,3,2), ("s",0,3),
-    ("s",1,1), ("w",2,0,2), ("w",1,7,3), ("src",2,2), ("t",0,5), ("w",0,5,0), ("t",3,4), ("t",1,2),
-    ("w",0,6,2), ("t",1,3), ("w",0,7,0), ("w",0,5,2), ("w",2,6,0), ("sib",0,2), ("t",2,3), ("w",2,3,0),
-    ("w",0,3,3), ("w",0,1,3), ("w",1,7,0), ("t",2,4), ("w",1,2,1), ("s",1,2), ("sib",2,0), ("s",3,3),
-    ("sib",2,1), ("w",1,1,1), ("dots",0,(0,1,2,3,4),0), ("t",0,7), ("w",1,5,2), ("s",3,1), ("t",3,7),
-    ("sib",0,3), ("w",0,5,1), ("w",0,8,1), ("t",3,0), ("dots",0,(0,1,2),1), ("t",1,4), ("w",0,6,0),
-    ("t",3,1), ("sib",1,0), ("w",1,6,2), ("sib",1,1), ("t",2,5), ("s",2,0), ("s",0,2), ("w",0,8,0),
-    ("w",0,6,1), ("w",2,3,3), ("s",0,0), ("sib",3,0), ("sib",0,1), ("w",0,7,2), ("t",3,5), ("s",3,2),
-    ("t",1,5), ("w",0,8,2), ("t",3,6), ("w",0,6,3), ("sib",3,2), ("w",2,7,1), ("w",2,1,2), ("t",3,3),
-    ("w",2,1,1), ("w",2,2,2), ("w",1,3,3), ("w",2,2,1), ("dots",0,(5,6),0), ("sib",2,2), ("t",1,6),
-    ("t",3,2), ("sib",3,1), ("sib",1,2), ("sib",3,3), ("t",2,6), ("t",1,7), ("sib",1,3), ("t",2,7),
-    ("w",2,5,3), ("s",0,1), ("w",1,4,1), ("w",1,3,1), ("sib",2,3), ("w",1,7,2), ("w",1,8,2), ("s",1,3),
-    ("dots",1,(0,1,2,3,4,5,6),0), ("w",2,4,2), ("w",0,8,3), ("w",2,3,2), ("w",0,7,1), ("dots",1,(7,),0),
-    ("w",1,6,0), ("kv",1), ("w",1,6,3), ("w",2,3,1), ("w",1,8,0), ("w",2,4,1), ("dots",1,(0,1,2,3,4),1),
-    ("w",1,5,0), ("w",1,6,1), ("dots",0,(7,),0), ("w",1,5,1), ("kv",0), ("w",2,2,3), ("w",2,5,2),
-    ("w",2,6,2), ("dots",1,(5,6),1), ("w",2,5,1), ("w",1,7,1), ("dots",0,(0,1,2),2), ("w",2,5,0),
-    ("dots",0,(3,4),1), ("w",1,8,3), ("w",1,8,1), ("dots",1,(7,),1), ("q",1), ("w",2,6,1),
-    ("dots",0,(5,6),1), ("w",2,8,2), ("dots",0,(7,),1), ("w",2,4,3), ("w",2,7,2), ("dots",1,(0,1,2,3,4),2),
-    ("w",2,6,3), ("dots",0,(3,4),2), ("w",2,8,3), ("dots",1,(5,6),2), ("w",2,7,3), ("w",2,8,1),
-    ("dots",1,(7,),2), ("q",2), ("dots",0,(5,6),2), ("qin",1,0), ("dots",0,(7,),2), ("kvin",), ("qin",1,1),
-    ("att",1,1), ("att",0,2), ("att",0,1), ("qin",2,0), ("att",1,2,0), ("qin",2,1), ("att",1,2,1),
+    ("w",0,2,3), ("w",2,8,0), ("w",0,5,3), ("w",2,5,3), ("pair",0), ("s",3,2), ("w",1,1,3), ("s",2,3),
+    ("near",0), ("pair",1), ("src",2,0), ("near",2), ("s",1,0), ("tables",1), ("pair",2), ("s",1,2),
+    ("src",0,0), ("src",1,0), ("w",0,0,2), ("src",0,2), ("w",1,2,3), ("tokp",3), ("tokp",0), ("near",1),
+    ("w",0,8,0), ("w",0,2,0), ("w",1,0,2), ("src",1,2), ("w",2,0,2), ("w",0,0,1), ("w",2,7,0), ("src",0,1),
+    ("w",2,0,1), ("w",0,1,0), ("tokp",2), ("src",2,2), ("w",1,2,0), ("tokp",1), ("w",2,1,0), ("w",0,0,3),
+    ("s",2,0), ("t",0,3), ("s",1,1), ("w",0,1,2), ("tokp",4), ("t",0,0), ("w",0,2,2), ("w",2,2,0),
+    ("w",1,1,2), ("w",1,1,0), ("w",1,0,1), ("s",0,0), ("w",1,2,2), ("w",1,3,3), ("tokp",7), ("w",0,3,0),
+    ("tokp",6), ("t",0,2), ("w",0,1,1), ("s",0,3), ("t",0,1), ("src",1,1), ("tokp2",6), ("w",1,3,2),
+    ("w",0,2,1), ("tokp",5), ("s",3,1), ("w",0,3,2), ("s",2,1), ("w",0,4,2), ("src",2,1), ("t",1,0),
+    ("t",0,4), ("tokp2",7), ("t",2,2), ("t",2,3), ("s",3,0), ("w",0,4,0), ("w",1,4,2), ("s",2,2),
+    ("w",1,4,0), ("t",1,1), ("w",0,3,1), ("w",2,1,2), ("tokp2",5), ("w",2,0,3), ("w",1,1,1), ("tokp2",4),
+    ("w",0,6,2), ("w",0,4,1), ("s",1,3), ("w",2,7,1), ("w",2,3,3), ("w",1,2,1), ("w",0,7,1), ("t",0,6),
+    ("sib",0,0), ("w",1,8,0), ("t",0,7), ("w",1,0,3), ("w",2,2,2), ("w",2,7,3), ("w",0,5,2), ("w",1,5,2),
+    ("w",1,3,0), ("w",2,2,1), ("t",0,5), ("w",1,8,3), ("sib",1,0), ("tables",0), ("w",2,1,1), ("w",1,7,1),
+    ("t",1,6), ("t",1,2), ("s",0,1), ("t",3,3), ("t",3,5), ("w",0,5,0), ("t",3,2), ("s",3,3), ("sib",0,2),
+    ("t",1,3), ("t",2,4), ("t",3,0), ("sib",3,1), ("t",2,6), ("w",0,5,1), ("w",2,2,3), ("w",1,6,2),
+    ("sib",1,1), ("w",0,8,2), ("t",3,1), ("t",1,4), ("t",2,1), ("w",0,6,1), ("w",0,3,3), ("sib",3,0),
+    ("w",0,7,3), ("w",0,1,3), ("sib",0,1), ("t",3,4), ("w",0,6,0), ("sib",3,2), ("w",2,3,2), ("t",2,7),
+    ("w",1,6,0), ("w",1,7,0), ("sib",2,3), ("w",2,1,3), ("w",1,3,1), ("t",1,7), ("sib",2,1), ("sib",0,3),
+    ("t",3,7), ("t",1,5), ("w",0,7,2), ("t",2,5), ("t",3,6), ("sib",2,2), ("t",2,0), ("w",1,4,1),
+    ("w",0,6,3), ("sib",2,0), ("sib",3,3), ("w",0,4,3), ("sib",1,3), ("w",1,7,2), ("sib",1,2), ("w",1,6,3),
+    ("w",1,4,3), ("dots",0,(0,1,2),1), ("dots",0,(0,1,2,3,4),0), ("dots",0,(5,6),0), ("w",2,4,2),
+    ("dots",0,(0,1,2),2), ("w",2,3,1), ("w",1,5,3), ("w",1,5,0), ("w",1,8,2), ("w",2,3,0), ("w",0,8,1),
+    ("s",0,2), ("dots",1,(0,1,2,3,4,5,6),0), ("w",0,8,3), ("w",0,7,0), ("w",2,4,1), ("dots",1,(7,),0),
+    ("kv",1), ("w",1,6,1), ("w",1,5,1), ("w",2,5,2), ("w",2,6,2), ("dots",0,(7,),0), ("kv",0), ("w",2,4,0),
+    ("dots",1,(0,1,2,3,4),1), ("dots",0,(3,4),1), ("dots",1,(5,6),1), ("w",2,5,1), ("w",1,7,3), ("w",2,8,2),
+    ("w",2,4,3), ("w",2,5,0), ("w",1,8,1), ("dots",1,(7,),1), ("w",2,7,2), ("w",2,6,1), ("q",1), ("w",2,6,0),
+    ("dots",0,(5,6),1), ("dots",0,(3,4),2), ("dots",0,(7,),1), ("w",2,6,3), ("dots",0,(5,6),2),
+    ("dots",1,(0,1,2,3,4),2), ("dots",1,(5,6),2), ("w",2,8,3), ("w",2,8,1), ("dots",1,(7,),2), ("q",2),
+    ("dots",0,(7,),2), ("kvin",), ("att",0,2), ("att",0,1), ("qin",1,0), ("qin",1,1), ("att",1,1),
+    ("qin",2,0), ("att",1,2,0), ("qin",2,1), ("att",1,2,1),
 )
 
 
@@ -424,6 +424,8 @@
     freq = jnp.asarray(np.concatenate([half, half])[None, :])
     any_ = pl.BlockSpec(memory_space=pl.ANY)
     dma = pltpu.SemaphoreType.DMA
+    operands = (tokens, q_weight, kv_weight, q_gain[None, :], k_gain[None, :], freq, doc_lengths.T)
+    operands = [pltpu.with_memory_space_constraint(a, pltpu.HBM) for a in operands]
     return pl.pallas_call(
         kernel,
         out_shape=jax.ShapeDtypeStruct((ROWS, 1024), BF16),
@@ -457,10 +459,10 @@
             dma((8,)),
         ],
         compiler_params=pltpu.CompilerParams(
-            collective_id=0, has_side_effects=True, vmem_limit_bytes=60 * 2**20),
+            collective_id=0, has_side_effects=True, vmem_limit_bytes=24 * 2**20),
         cost_estimate=pl.CostEstimate(
             flops=6_000_000_000, bytes_accessed=12 * 2**20, transcendentals=2**21),
-    )(tokens, q_weight, kv_weight, q_gain[None, :], k_gain[None, :], freq, doc_lengths.T)
+    )(*operands)
 
 
 def solution(mesh):

time: 63.2 us -> 60.1 us (0.951)
  Pallas kernels: 60.8 us -> 59.1 us
  local copies, waits for them, and re-layouts: 2.26 us -> 0.97 us
    pallas_call x1, Pallas kernels: 60.8 us -> 59.1 us  [shards(): pl.pallas_call(kernel, out_shape=jax.ShapeDtypeStruct((ROWS, 1024), BF16)...]
    unnamed x1, local copies, waits for them, and re-layouts: 2.26 us -> 0.97 us
where the time goes in v4:
time: 60.1 us
  Pallas kernels  59.1 us (98%)
  local copies, waits for them, and re-layouts  0.97 us (2%)
    pallas_call x1, Pallas kernels, shards(): pl.pallas_call(kernel, out_shape=jax.ShapeDtypeStruct((ROWS, 1024), BF16)...  59.1 us

profile of v4, /device:TPU:1, one launch (start us, length us, event | category | flops | bytes accessed | tf_op | source)
XLA Modules:
  0.0 60.1 jit_solution(11568494405110387888)
XLA Ops:
  0.0 59.1 %shard_map.73 = bf16[512,1024]{1,0:T(8,128)(2,1)S(1)} custom-call(bf16[512,4096]{1,0:T(8,128)(2,1)} %tok.1, bf16[128,1024]{1,0:T(8,128)(2,1)} %w.1, bf16[128,128]{1,0:T(8,128)(2,1)} %kvw.1, f32[1,128]{1,0:T(1,128)} %bitcast.4, f32[1,128]{1,0:T(1,128)} %bitcast.5, f32[1,128]{1,0:T(1,128)} %constant.2.clone.freq_in, s32[16,32]{1,0:T(8,128)} %bitcast.3), custom_call_target="tpu_custom_call" | custom-call | flops 6000000000 | bytes 12582912 | tf_op jit(solution)/shard_map/pallas_call | solution.py:429
  59.1 1.0 %copy.9 = bf16[512,1024]{1,0:T(8,128)(2,1)} copy(bf16[512,1024]{1,0:T(8,128)(2,1)S(1)} %shard_map.73) | data formatting | bytes 2097152

commit v5 on v4

--- a/solution.py
+++ b/solution.py
@@ -51,10 +51,10 @@
     ("dots",0,(0,1,2),2), ("w",2,3,1), ("w",1,5,3), ("w",1,5,0), ("w",1,8,2), ("w",2,3,0), ("w",0,8,1),
     ("s",0,2), ("dots",1,(0,1,2,3,4,5,6),0), ("w",0,8,3), ("w",0,7,0), ("w",2,4,1), ("dots",1,(7,),0),
     ("kv",1), ("w",1,6,1), ("w",1,5,1), ("w",2,5,2), ("w",2,6,2), ("dots",0,(7,),0), ("kv",0), ("w",2,4,0),
-    ("dots",1,(0,1,2,3,4),1), ("dots",0,(3,4),1), ("dots",1,(5,6),1), ("w",2,5,1), ("w",1,7,3), ("w",2,8,2),
-    ("w",2,4,3), ("w",2,5,0), ("w",1,8,1), ("dots",1,(7,),1), ("w",2,7,2), ("w",2,6,1), ("q",1), ("w",2,6,0),
-    ("dots",0,(5,6),1), ("dots",0,(3,4),2), ("dots",0,(7,),1), ("w",2,6,3), ("dots",0,(5,6),2),
-    ("dots",1,(0,1,2,3,4),2), ("dots",1,(5,6),2), ("w",2,8,3), ("w",2,8,1), ("dots",1,(7,),2), ("q",2),
+    ("dots",1,(0,1,2,3,4),1), ("dots",1,(5,6),1), ("w",2,5,1), ("w",1,7,3), ("w",2,4,3), ("w",2,5,0),
+    ("w",1,8,1), ("dots",1,(7,),1), ("w",2,7,2), ("w",2,6,1), ("q",1), ("w",2,8,2), ("dots",0,(3,4),1),
+    ("w",2,6,0), ("dots",0,(3,4),2), ("w",2,6,3), ("dots",1,(0,1,2,3,4),2), ("dots",1,(5,6),2), ("w",2,8,3),
+    ("w",2,8,1), ("dots",1,(7,),2), ("q",2), ("dots",0,(5,6),2), ("dots",0,(5,6),1), ("dots",0,(7,),1),
     ("dots",0,(7,),2), ("kvin",), ("att",0,2), ("att",0,1), ("qin",1,0), ("qin",1,1), ("att",1,1),
     ("qin",2,0), ("att",1,2,0), ("qin",2,1), ("att",1,2,1),
 )

time: 60.1 us -> 60.1 us (level)
  no operation moved by 1% of the time
where the time goes in v5:
time: 60.1 us
  Pallas kernels  59.1 us (98%)
  local copies, waits for them, and re-layouts  0.97 us (2%)
    pallas_call x1, Pallas kernels, shards(): pl.pallas_call(kernel, out_shape=jax.ShapeDtypeStruct((ROWS, 1024), BF16)...  59.1 us

profile of v5, /device:TPU:1, one launch (start us, length us, event | category | flops | bytes accessed | tf_op | source)
XLA Modules:
  0.0 60.1 jit_solution(14187803278093587743)
XLA Ops:
  0.0 59.1 %shard_map.73 = bf16[512,1024]{1,0:T(8,128)(2,1)S(1)} custom-call(bf16[512,4096]{1,0:T(8,128)(2,1)} %tok.1, bf16[128,1024]{1,0:T(8,128)(2,1)} %w.1, bf16[128,128]{1,0:T(8,128)(2,1)} %kvw.1, f32[1,128]{1,0:T(1,128)} %bitcast.4, f32[1,128]{1,0:T(1,128)} %bitcast.5, f32[1,128]{1,0:T(1,128)} %constant.2.clone.freq_in, s32[16,32]{1,0:T(8,128)} %bitcast.3), custom_call_target="tpu_custom_call" | custom-call | flops 6000000000 | bytes 12582912 | tf_op jit(solution)/shard_map/pallas_call | solution.py:429
  59.1 1.0 %copy.9 = bf16[512,1024]{1,0:T(8,128)(2,1)} copy(bf16[512,1024]{1,0:T(8,128)(2,1)S(1)} %shard_map.73) | data formatting | bytes 2097152

commit v6 on v4

--- a/solution.py
+++ b/solution.py
@@ -61,7 +61,7 @@
 
 
 def kernel(tok, w, kvw, qg_in, kg_in, freq_in, dl_in, out,
-           tokb, wbuf, kvbuf, stage, acc, kvacc, kvst, kvin, cosb, sinb, bias, ost, qst, qin, qg, kg, freq, dl,
+           tokb, wbuf, kvbuf, stage, acc, kvacc, kvst, kvin, cosb, sinb, bias, ost, qst, qin, own, qg, kg, freq, dl,
            send, rw, rt, rs, rkv, rq, loc):
     dp = lax.axis_index("dp")
     hd = lax.axis_index("head")
@@ -306,7 +306,7 @@
 
     def query(t, g, hh):
         u = acc[t, g - 1, :, 128 * hh:128 * hh + 128]
-        return norm_rope(u, qg[...], t, by_matrix_unit=t == 0)
+        return norm_rope(u, qg[...], t, by_matrix_unit=False)
 
     def send_queries(g):
         for hh in (0, 1):
@@ -316,7 +316,7 @@
 
     def attend(of, g, hh):
         n = 2 * (g - 1) + hh
-        q = query(0, g, hh) if of == 0 else qin[n]
+        q = own[n] if of == 0 else qin[n]
         for i in (0, 1):
             m = 256 * (i + 1)
             s = lax.dot_general(q[256 * i:m], kvin[0, :m], (((1,), (1,)), ((), ())),
@@ -385,6 +385,8 @@
             kv_finish(*a)
             kv_send(*a)
         elif what == "kvin":
+            for n in range(4):
+                own[n] = query(0, 1 + n // 2, n % 2)
             kv_arrived()
         elif what == "q":
             send_queries(*a)
@@ -446,6 +448,7 @@
             pltpu.VMEM((2, ROWS, 512), BF16),
             pltpu.VMEM((4, ROWS, HD), BF16),
             pltpu.VMEM((4, ROWS, HD), BF16),
+            pltpu.VMEM((4, ROWS, HD), BF16),
             pltpu.VMEM((1, HD), F32),
             pltpu.VMEM((1, HD), F32),
             pltpu.VMEM((1, HD), F32),

time: 60.1 us -> 60.1 us (level)
  no operation moved by 1% of the time
where the time goes in v6:
time: 60.1 us
  Pallas kernels  59.1 us (98%)
  local copies, waits for them, and re-layouts  0.97 us (2%)
    pallas_call x1, Pallas kernels, shards(): pl.pallas_call(kernel, out_shape=jax.ShapeDtypeStruct((ROWS, 1024), BF16)...  59.1 us

profile of v6, /device:TPU:1, one launch (start us, length us, event | category | flops | bytes accessed | tf_op | source)
XLA Modules:
  0.0 60.1 jit_solution(9166216529593904254)
XLA Ops:
  0.0 59.1 %shard_map.73 = bf16[512,1024]{1,0:T(8,128)(2,1)S(1)} custom-call(bf16[512,4096]{1,0:T(8,128)(2,1)} %tok.1, bf16[128,1024]{1,0:T(8,128)(2,1)} %w.1, bf16[128,128]{1,0:T(8,128)(2,1)} %kvw.1, f32[1,128]{1,0:T(1,128)} %bitcast.4, f32[1,128]{1,0:T(1,128)} %bitcast.5, f32[1,128]{1,0:T(1,128)} %constant.2.clone.freq_in, s32[16,32]{1,0:T(8,128)} %bitcast.3), custom_call_target="tpu_custom_call" | custom-call | flops 6000000000 | bytes 12582912 | tf_op jit(solution)/shard_map/pallas_call | solution.py:431
  59.1 1.0 %copy.9 = bf16[512,1024]{1,0:T(8,128)(2,1)} copy(bf16[512,1024]{1,0:T(8,128)(2,1)S(1)} %shard_map.73) | data formatting | bytes 2097152
